TPU v7x, 512 devices: a whole 4x8x8 slice. The times are simulated.
512 devices in a mesh: seq: 64 (over z_hi, x, y), tp: 8 (over z_lo, core).
Axes of the slice: x: 4, y: 8, z: 8 (z_hi: 2, z_lo: 4; z = z_hi * 4 + z_lo), core: 2. Of those that a mesh axis runs over, the one named last changes fastest.
Arguments:
- features: bfloat16 [8192, 8192], P('seq', 'tp'), may hold values from -6 to 6
- in_proj: bfloat16 [3, 8192, 1024], P(None, 'seq', 'tp'), may hold values from -0.0625 to 0.0625
- short_taps: float32 [3, 3, 1024], P(None, None, 'tp'), may hold values from -3 to 3
- long_filter: float32 [8192, 1024], P('seq', 'tp'), may hold values from -1.8 to 1.8
- skip_gain: float32 [1024], P('tp'), may hold values from -4 to 4
- out_proj: bfloat16 [1024, 8192], P('tp', 'seq'), may hold values from -0.1875 to 0.1875
Outputs:
- mixed: bfloat16 [8192, 8192], P('seq', 'tp')
All inputs are finite; a program needn't handle non-finite values.
Results may differ from a plain program's by a relative error of at most 0.007.
Values may be sent and summed in bfloat16 or wider, within the bound.
A program may use at most 64 MiB of HBM per device.

v0:
```python
import math

import jax
import jax.numpy as jnp
from jax import lax
from jax.sharding import PartitionSpec as P

HIGHEST = lax.Precision.HIGHEST


def from_behind(array, axis, by):
    count = lax.axis_size(axis)
    pairs = [(i, i + by) for i in range(count) if 0 <= i + by < count]
    return lax.ppermute(array, axis, pairs)


def contract(form, table, values):
    return jnp.einsum(form, table, values, precision=HIGHEST, preferred_element_type=jnp.float32)


def complex_apply(form, tab_real, tab_imag, in_real, in_imag):
    out_real = contract(form, tab_real, in_real) - contract(form, tab_imag, in_imag)
    out_imag = contract(form, tab_real, in_imag) + contract(form, tab_imag, in_real)
    return (out_real, out_imag)


def phases(first, second, modulus, sign):
    product = first[:, None] * second[None, :] % modulus
    angle = sign * 2.0 * math.pi / modulus * product.astype(jnp.float32)
    return (jnp.cos(angle), jnp.sin(angle))


def split_factor(total):
    first_len = 1
    for cand in range(1, total + 1):
        if cand * cand > total:
            break
        if total % cand == 0:
            first_len = cand
    return (first_len, total // first_len)


def local_forward(in_real, in_imag):
    count, tok_rows, chan_dev = in_real.shape
    first_len, second_len = split_factor(tok_rows)
    in_real = in_real.reshape(count, first_len, second_len, chan_dev)
    in_imag = in_imag.reshape(count, first_len, second_len, chan_dev)
    index_first = jnp.arange(first_len, dtype=jnp.int32)
    index_second = jnp.arange(second_len, dtype=jnp.int32)
    tab_real, tab_imag = phases(index_first, index_first, first_len, -1.0)
    mid_real, mid_imag = complex_apply("ma,qabc->qmbc", tab_real, tab_imag, in_real, in_imag)
    turn_real, turn_imag = phases(index_first, index_second, tok_rows, -1.0)
    turn_real = turn_real[None, :, :, None]
    turn_imag = turn_imag[None, :, :, None]
    mid_real, mid_imag = (
        mid_real * turn_real - mid_imag * turn_imag,
        mid_real * turn_imag + mid_imag * turn_real,
    )
    tab_real, tab_imag = phases(index_second, index_second, second_len, -1.0)
    out_real, out_imag = complex_apply("nb,qmbc->qmnc", tab_real, tab_imag, mid_real, mid_imag)
    return (
        out_real.reshape(count, tok_rows, chan_dev),
        out_imag.reshape(count, tok_rows, chan_dev),
    )


def local_inverse(in_real, in_imag):
    count, tok_rows, chan_dev = in_real.shape
    first_len, second_len = split_factor(tok_rows)
    in_real = in_real.reshape(count, first_len, second_len, chan_dev)
    in_imag = in_imag.reshape(count, first_len, second_len, chan_dev)
    index_first = jnp.arange(first_len, dtype=jnp.int32)
    index_second = jnp.arange(second_len, dtype=jnp.int32)
    tab_real, tab_imag = phases(index_second, index_second, second_len, 1.0)
    mid_real, mid_imag = complex_apply("bn,qmnc->qmbc", tab_real, tab_imag, in_real, in_imag)
    turn_real, turn_imag = phases(index_first, index_second, tok_rows, 1.0)
    turn_real = turn_real[None, :, :, None]
    turn_imag = turn_imag[None, :, :, None]
    mid_real, mid_imag = (
        mid_real * turn_real - mid_imag * turn_imag,
        mid_real * turn_imag + mid_imag * turn_real,
    )
    tab_real, tab_imag = phases(index_first, index_first, first_len, 1.0)
    out_real, out_imag = complex_apply("am,qmbc->qabc", tab_real, tab_imag, mid_real, mid_imag)
    return (
        out_real.reshape(count, tok_rows, chan_dev),
        out_imag.reshape(count, tok_rows, chan_dev),
    )


def long_convolve(inner, long_filter):
    tok_rows, chan_dev = inner.shape
    seq_parts = lax.axis_size("seq")
    position = lax.axis_index("seq")
    seq_rows = tok_rows // seq_parts
    freq_count = 2 * seq_parts
    pad_length = 2 * tok_rows * seq_parts
    sent_inner, sent_filter = (
        lax.all_to_all(inner[None], "seq", split_axis=1, concat_axis=0, tiled=True),
        lax.all_to_all(long_filter[None], "seq", split_axis=1, concat_axis=0, tiled=True),
    )
    freq_index = jnp.arange(freq_count, dtype=jnp.int32)
    block_index = jnp.arange(seq_parts, dtype=jnp.int32)
    tab_real, tab_imag = phases(freq_index, block_index, freq_count, -1.0)
    inner_real = contract("qp,prc->qrc", tab_real, sent_inner)
    inner_imag = contract("qp,prc->qrc", tab_imag, sent_inner)
    filter_real = contract("qp,prc->qrc", tab_real, sent_filter)
    filter_imag = contract("qp,prc->qrc", tab_imag, sent_filter)
    global_rows = position * seq_rows + jnp.arange(seq_rows, dtype=jnp.int32)
    turn_real, turn_imag = phases(freq_index, global_rows, pad_length, -1.0)
    turn_real = turn_real[:, :, None]
    turn_imag = turn_imag[:, :, None]
    inner_real, inner_imag = (
        inner_real * turn_real - inner_imag * turn_imag,
        inner_real * turn_imag + inner_imag * turn_real,
    )
    filter_real, filter_imag = (
        filter_real * turn_real - filter_imag * turn_imag,
        filter_real * turn_imag + filter_imag * turn_real,
    )
    inner_real, inner_imag, filter_real, filter_imag = (
        lax.all_to_all(inner_real, "seq", split_axis=0, concat_axis=1, tiled=True),
        lax.all_to_all(inner_imag, "seq", split_axis=0, concat_axis=1, tiled=True),
        lax.all_to_all(filter_real, "seq", split_axis=0, concat_axis=1, tiled=True),
        lax.all_to_all(filter_imag, "seq", split_axis=0, concat_axis=1, tiled=True),
    )
    spec_real, spec_imag = local_forward(
        jnp.concatenate([inner_real, filter_real], 0), jnp.concatenate([inner_imag, filter_imag], 0)
    )
    pair = inner_real.shape[0]
    left_real, right_real = (spec_real[:pair], spec_real[pair:])
    left_imag, right_imag = (spec_imag[:pair], spec_imag[pair:])
    prod_real = left_real * right_real - left_imag * right_imag
    prod_imag = left_real * right_imag + left_imag * right_real
    back_real, back_imag = local_inverse(prod_real, prod_imag)
    back_real, back_imag = (
        lax.all_to_all(back_real, "seq", split_axis=1, concat_axis=0, tiled=True),
        lax.all_to_all(back_imag, "seq", split_axis=1, concat_axis=0, tiled=True),
    )
    back_real, back_imag = (
        back_real * turn_real + back_imag * turn_imag,
        back_imag * turn_real - back_real * turn_imag,
    )
    inv_real, inv_imag = phases(block_index, freq_index, freq_count, 1.0)
    values = (
        contract("pq,qrc->prc", inv_real, back_real) - contract("pq,qrc->prc", inv_imag, back_imag)
    ) / pad_length
    result = lax.all_to_all(values, "seq", split_axis=0, concat_axis=1, tiled=True)
    return result[0]


def per_device(features, in_proj, short_taps, long_filter, skip_gain, out_proj):
    tok_rows = features.shape[0]
    chan_dev = in_proj.shape[2]
    taps_count = short_taps.shape[1]
    full_in = lax.all_gather(in_proj, "seq", axis=1, tiled=True)
    full_out = lax.all_gather(out_proj, "seq", axis=1, tiled=True)
    empty = jnp.zeros((3, tok_rows, chan_dev), jnp.float32)
    piece = jax.tree.map(lambda part: lax.all_gather(part, "tp", axis=1, tiled=True), features)
    weight_rows = lax.slice_in_dim(full_in, 0, piece.shape[1], axis=1)
    projected = (
        empty + jnp.einsum("tk,skc->stc", piece, weight_rows, preferred_element_type=jnp.float32)
    ).astype(jnp.bfloat16)
    earlier = from_behind(projected[:, tok_rows - (taps_count - 1) :, :], "seq", 1)
    padded = jnp.concatenate([earlier, projected], axis=1).astype(jnp.float32)
    filtered = jnp.zeros((3, tok_rows, chan_dev), jnp.float32)
    for offset in range(taps_count):
        begin = taps_count - 1 - offset
        filtered = (
            filtered + short_taps[:, offset, None, :] * padded[:, begin : begin + tok_rows, :]
        )
    query = filtered[0]
    inner = filtered[1] * filtered[2]
    long_mix = long_convolve(inner, long_filter)
    gated = (query * (long_mix + skip_gain[None, :] * inner)).astype(jnp.bfloat16)
    terms = jnp.dot(gated, full_out, preferred_element_type=jnp.float32)
    mixed = lax.psum_scatter(terms, "tp", scatter_dimension=1, tiled=True)
    return mixed.astype(jnp.bfloat16)


def solution(mesh):
    return jax.shard_map(
        per_device,
        mesh=mesh,
        in_specs=(
            P("seq", "tp"),
            P(None, "seq", "tp"),
            P(None, None, "tp"),
            P("seq", "tp"),
            P("tp"),
            P("tp", "seq"),
        ),
        out_specs=P("seq", "tp"),
        check_vma=False,
    )
```

profile of v0, /device:TPU:1, one launch (start us, length us, event | category | flops | bytes accessed | tf_op | source)
XLA Modules:
  0.0 526.2 jit_solution(7247148806284053348)
XLA Ops:
  6.5 0.7 all-gather.6.cloned.1.call-update
  8.0 19.6 %all-to-all-start.2 = ((f32[1,128,128]{2,0,1:T(1,128)}), f32[1,128,128]{2,0,1:T(1,128)S(1)}, u32[]{:S(2)}, u32[]{:S(2)}) async-start(f32[1,128,128]{2,0,1:T(1,128)} %bitcast.186), calls=%async_computation.2 | async-start | bytes 131072 | tf_op jit(solution)/shard_map/all_to_all | solution.py:100
  27.6 0.8 fusion.242
  28.4 27.7 %all-gather.6.cloned.1.call-done = bf16[128,8192]{1,0:T(8,128)(2,1)} async-done(((bf16[128,1024]{1,0:T(8,128)(2,1)}), bf16[128,8192]{1,0:T(8,128)(2,1)}) %all-gather.6.cloned.1.call-update) | async-done | bytes 2097168 | tf_op jit(solution)/shard_map/all_gather | solution.py:159
  56.1 180.4 %all-gather.4.cloned.1.call-done = bf16[3,8192,128]{2,1,0:T(8,128)(2,1)} async-done(((bf16[3,128,128]{2,1,0:T(8,128)(2,1)}), bf16[3,8192,128]{2,1,0:T(8,128)(2,1)}) %all-gather.4.cloned.1.call-update) | async-done | bytes 6291472 | tf_op jit(solution)/shard_map/all_gather | solution.py:156
  236.5 4.7 fusion.11
  241.2 2.7 collective-permute-start
  245.3 10.7 %all-to-all-start = ((f32[1,128,128]{2,0,1:T(1,128)}), f32[1,128,128]{2,0,1:T(1,128)S(1)}, u32[]{:S(2)}, u32[]{:S(2)}) async-start(f32[1,128,128]{2,0,1:T(1,128)} %bitcast.5), calls=%async_computation | async-start | bytes 131072 | tf_op jit(solution)/shard_map/all_to_all | solution.py:99
  256.5 13.0 %all-to-all-done = f32[1,128,128]{2,0,1:T(1,128)S(1)} async-done(((f32[1,128,128]{2,0,1:T(1,128)}), f32[1,128,128]{2,0,1:T(1,128)S(1)}, u32[]{:S(2)}, u32[]{:S(2)}) %all-to-all-start) | async-done | bytes 65568 | tf_op jit(solution)/shard_map/all_to_all | solution.py:99
  270.8 0.8 copy.124
  271.6 4.6 all-to-all-start.3
  276.2 0.7 copy.130
  276.9 13.2 %all-to-all-done.3 = f32[128,2,128]{2,1,0:T(2,128)S(1)} async-done(((f32[128,2,128]{2,1,0:T(2,128)}), f32[128,2,128]{2,1,0:T(2,128)S(1)}, u32[]{:S(2)}, u32[]{:S(2)}) %all-to-all-start.3) | async-done | bytes 131104 | tf_op jit(solution)/shard_map/all_to_all | solution.py:124
  290.1 4.6 all-to-all-start.5
  294.7 0.7 copy.128
  295.5 13.2 %all-to-all-done.5 = f32[128,2,128]{2,1,0:T(2,128)S(1)} async-done(((f32[128,2,128]{2,1,0:T(2,128)}), f32[128,2,128]{2,1,0:T(2,128)S(1)}, u32[]{:S(2)}, u32[]{:S(2)}) %all-to-all-start.5) | async-done | bytes 131104 | tf_op jit(solution)/shard_map/all_to_all | solution.py:125
  308.6 4.6 all-to-all-start.4
  314.1 0.8 copy.120
  314.8 12.3 %all-to-all-done.4 = f32[128,2,128]{2,1,0:T(2,128)S(1)} async-done(((f32[128,2,128]{2,1,0:T(2,128)}), f32[128,2,128]{2,1,0:T(2,128)S(1)}, u32[]{:S(2)}, u32[]{:S(2)}) %all-to-all-start.4) | async-done | bytes 131104 | tf_op jit(solution)/shard_map/all_to_all | solution.py:123
  327.1 4.8 all-to-all-start.1
  332.3 13.3 %all-to-all-done.1 = f32[128,2,128]{2,1,0:T(2,128)S(1)} async-done(((f32[128,2,128]{2,1,0:T(2,128)}), f32[128,2,128]{2,1,0:T(2,128)S(1)}, u32[]{:S(2)}, u32[]{:S(2)}) %all-to-all-start.1) | async-done | bytes 131104 | tf_op jit(solution)/shard_map/all_to_all | solution.py:122
  351.2 0.7 copy.143
  352.0 4.6 all-to-all-start.6
  357.2 0.8 copy.149
  358.0 12.9 %all-to-all-done.6 = f32[2,128,128]{2,0,1:T(2,128)S(1)} async-done(((f32[2,128,128]{2,0,1:T(2,128)}), f32[2,128,128]{2,0,1:T(2,128)S(1)}, u32[]{:S(2)}, u32[]{:S(2)}) %all-to-all-start.6) | async-done | bytes 131104 | tf_op jit(solution)/shard_map/all_to_all | solution.py:137
  370.9 4.6 all-to-all-start.7
  375.7 13.8 %all-to-all-done.7 = f32[2,128,128]{2,0,1:T(2,128)S(1)} async-done(((f32[2,128,128]{2,0,1:T(2,128)}), f32[2,128,128]{2,0,1:T(2,128)S(1)}, u32[]{:S(2)}, u32[]{:S(2)}) %all-to-all-start.7) | async-done | bytes 131104 | tf_op jit(solution)/shard_map/all_to_all | solution.py:138
  391.0 4.6 all-to-all-start.8
  395.7 66.0 %all-gather.8.cloned.1.call-done = bf16[128,8192]{1,0:T(8,128)(2,1)} async-done(((bf16[128,128]{1,0:T(8,128)(2,1)}), bf16[128,8192]{1,0:T(8,128)(2,1)}) %all-gather.8.cloned.1.call-update) | async-done | bytes 2097168 | tf_op jit(solution)/shard_map/all_gather | solution.py:157
  461.7 4.3 fusion.57
  466.0 51.9 %reduce-scatter.2.cloned.1.call-done = f32[128,1024]{1,0:T(8,128)} async-done(((f32[128,8192]{1,0:T(8,128)}), f32[128,1024]{1,0:T(8,128)}) %reduce-scatter.2.cloned.1.call-update) | async-done | bytes 524304 | tf_op jit(solution)/shard_map/reduce_scatter | solution.py:177
  517.9 1.8 convert_element_type.116
  (63 shorter events, 13.0 us)
Async XLA Ops:
  6.5 49.6 %all-gather.6.cloned.1.call-start = ((), (), s32[]{:S(2)}) async-start(), calls=%async_computation.11 | async-start | bytes 2359296 | tf_op jit(solution)/shard_map/all_gather | solution.py:159
  7.3 229.2 %all-gather.4.cloned.1.call-start = ((), (), s32[]{:S(2)}) async-start(), calls=%async_computation.10 | async-start | bytes 6389760 | tf_op jit(solution)/shard_map/all_gather | solution.py:156
  8.0 237.3 %all-to-all-start.2 = ((f32[1,128,128]{2,0,1:T(1,128)}), f32[1,128,128]{2,0,1:T(1,128)S(1)}, u32[]{:S(2)}, u32[]{:S(2)}) async-start(f32[1,128,128]{2,0,1:T(1,128)} %bitcast.186), calls=%async_computation.2 | async-start | bytes 131072 | tf_op jit(solution)/shard_map/all_to_all | solution.py:100
  241.2 3.4 collective-permute-start
  245.3 24.1 %all-to-all-start = ((f32[1,128,128]{2,0,1:T(1,128)}), f32[1,128,128]{2,0,1:T(1,128)S(1)}, u32[]{:S(2)}, u32[]{:S(2)}) async-start(f32[1,128,128]{2,0,1:T(1,128)} %bitcast.5), calls=%async_computation | async-start | bytes 131072 | tf_op jit(solution)/shard_map/all_to_all | solution.py:99
  271.6 18.5 %all-to-all-start.3 = ((f32[128,2,128]{2,1,0:T(2,128)}), f32[128,2,128]{2,1,0:T(2,128)S(1)}, u32[]{:S(2)}, u32[]{:S(2)}) async-start(f32[128,2,128]{2,1,0:T(2,128)} %copy.124), calls=%async_computation.3 | async-start | bytes 262144 | tf_op jit(solution)/shard_map/all_to_all | solution.py:124
  290.1 18.5 %all-to-all-start.5 = ((f32[128,2,128]{2,1,0:T(2,128)}), f32[128,2,128]{2,1,0:T(2,128)S(1)}, u32[]{:S(2)}, u32[]{:S(2)}) async-start(f32[128,2,128]{2,1,0:T(2,128)} %copy.130), calls=%async_computation.5 | async-start | bytes 262144 | tf_op jit(solution)/shard_map/all_to_all | solution.py:125
  308.6 18.5 %all-to-all-start.4 = ((f32[128,2,128]{2,1,0:T(2,128)}), f32[128,2,128]{2,1,0:T(2,128)S(1)}, u32[]{:S(2)}, u32[]{:S(2)}) async-start(f32[128,2,128]{2,1,0:T(2,128)} %copy.128), calls=%async_computation.4 | async-start | bytes 262144 | tf_op jit(solution)/shard_map/all_to_all | solution.py:123
  313.2 148.5 %all-gather.8.cloned.1.call-start = ((), (), s32[]{:S(2)}) async-start(), calls=%async_computation.12 | async-start | bytes 2129920 | tf_op jit(solution)/shard_map/all_gather | solution.py:157
  327.1 18.5 %all-to-all-start.1 = ((f32[128,2,128]{2,1,0:T(2,128)}), f32[128,2,128]{2,1,0:T(2,128)S(1)}, u32[]{:S(2)}, u32[]{:S(2)}) async-start(f32[128,2,128]{2,1,0:T(2,128)} %copy.120), calls=%async_computation.1 | async-start | bytes 262144 | tf_op jit(solution)/shard_map/all_to_all | solution.py:122
  351.2 110.5 %copy-start = (f32[128]{0:T(128)S(1)}, f32[128]{0:T(128)}, u32[]{:S(2)}) copy-start(f32[128]{0:T(128)} %param.10) | copy-start | bytes 1540
  352.0 18.9 %all-to-all-start.6 = ((f32[2,128,128]{2,0,1:T(2,128)}), f32[2,128,128]{2,0,1:T(2,128)S(1)}, u32[]{:S(2)}, u32[]{:S(2)}) async-start(f32[2,128,128]{2,0,1:T(2,128)} %copy.143), calls=%async_computation.6 | async-start | bytes 262144 | tf_op jit(solution)/shard_map/all_to_all | solution.py:137
  370.9 18.5 %all-to-all-start.7 = ((f32[2,128,128]{2,0,1:T(2,128)}), f32[2,128,128]{2,0,1:T(2,128)S(1)}, u32[]{:S(2)}, u32[]{:S(2)}) async-start(f32[2,128,128]{2,0,1:T(2,128)} %copy.149), calls=%async_computation.7 | async-start | bytes 262144 | tf_op jit(solution)/shard_map/all_to_all | solution.py:138
  391.0 70.6 %all-to-all-start.8 = ((f32[64,2,128]{2,1,0:T(2,128)}), f32[64,2,128]{2,1,0:T(2,128)S(1)}, u32[]{:S(2)}, u32[]{:S(2)}) async-start(f32[64,2,128]{2,1,0:T(2,128)} %copy.152), calls=%async_computation.8 | async-start | bytes 131072 | tf_op jit(solution)/shard_map/all_to_all | solution.py:148
  395.7 122.2 %reduce-scatter.2.cloned.1.call-start = ((), (), s32[]{:S(2)}) async-start(), calls=%async_computation.13 | async-start | bytes 4718592 | tf_op jit(solution)/shard_map/reduce_scatter | solution.py:177
Sparse Core Ops, SparseCore 0:
  9.4 46.6 all-gather.5
  60.5 175.9 all-gather.3
  318.3 143.2 all-gather.7
  466.1 51.6 reduce-scatter.1
where the time goes:
time: 529 us; the launch traced here: 526 us
  waiting for transfers between devices  420 us (79%)
  starting transfers between devices  65.6 us (12%)
  matrix products  17.3 us (3%)
  between operations  13.5 us (3%)
  local copies, waits for them, and re-layouts  6.82 us (1%)
    all_gather x1, waiting for transfers between devices, per_device(): full_in = lax.all_gather(in_proj, 'seq', axis=1, tiled=True)  180 us
    all_gather x1, waiting for transfers between devices, per_device(): full_out = lax.all_gather(out_proj, 'seq', axis=1, tiled=True)  66 us
    reduce_scatter x1, waiting for transfers between devices, per_device(): mixed = lax.psum_scatter(terms, 'tp', scatter_dimension=1, tiled=True)  51.9 us
    all_gather x1, waiting for transfers between devices, per_device(): lax.all_gather(part, 'tp', axis=1, tiled=True)  27.7 us
    all_to_all x1, starting transfers between devices, long_convolve(): lax.all_to_all(long_filter[None], 'seq', split_axis=1, concat_axis=0, til...  19.6 us
    all_to_all x1, waiting for transfers between devices, long_convolve(): lax.all_to_all(back_imag, 'seq', split_axis=1, concat_axis=0, tiled=True)  13.8 us
    all_to_all x1, waiting for transfers between devices, long_convolve(): lax.all_to_all(inner_real, 'seq', split_axis=0, concat_axis=1, tiled=True)  13.3 us
    all_to_all x1, waiting for transfers between devices, long_convolve(): lax.all_to_all(filter_real, 'seq', split_axis=0, concat_axis=1, tiled=True)  13.2 us
  transfers between devices with their start and end apart: 14, of which 12 were waited for; matrix products, arithmetic and copies ran while one was open for 4% of the time, Pallas kernels for 0%

commit v1 on v0

v1 whole, which is shorter than its diff:
```python
import functools

import jax
import jax.numpy as jnp
from jax import lax
from jax.experimental import pallas as pl
from jax.experimental.pallas import tpu as pltpu
from jax.sharding import PartitionSpec as P

B = 128
HALO = 16
BF16, F32 = jnp.bfloat16, jnp.float32


def lanes(i):
    return pl.ds(pl.multiple_of(i * B, B), B)


def kernel(
    ny, nx, feat, win, taps, filt, skip, wout, out,
    F, Wb, Wc, Ps, Pr, Hr, pad, qi, Fs, Fr, Xs, Xr, Ys, Yr, Xp, A, T, Gs, Gt, Wo,
    loc, sF, rF, sW, rW, sZ, rZ, sC, rC, sP, rP, sH, rH, sV, rV, sG, rG, sO, rO,
):
    np_ = 2 * nx
    nq = 2 * nx
    nzl = np_ // 2
    ns = nq * ny
    cpd = B // ns
    s = lax.axis_index("seq")
    p = lax.axis_index("tp")
    q, y = s // ny, s % ny
    zl, c = p // 2, p % 2
    mate = p + 1 - 2 * c
    far = (q + nx) % nq

    def send(src, dst, ss, rs, sq, tp):
        pltpu.make_async_remote_copy(
            src_ref=src, dst_ref=dst, send_sem=ss, recv_sem=rs,
            device_id={"seq": sq, "tp": tp}, device_id_type=pl.DeviceIdType.MESH,
        ).start()

    def wait(ref, sem):
        pltpu.make_async_copy(ref, ref, sem).wait()

    def local(src, dst, sem):
        pltpu.make_async_copy(src, dst, sem).start()

    def loop(lo, hi, body):
        lax.fori_loop(lo, hi, lambda i, carry: (body(i), carry)[1], 0)

    barrier = pltpu.get_barrier_semaphore()

    def greet(sq, tp):
        pl.semaphore_signal(
            barrier, inc=1, device_id={"seq": sq, "tp": tp}, device_id_type=pl.DeviceIdType.MESH
        )

    loop(1, ns, lambda k: greet((s + k) % ns, p))
    loop(1, np_, lambda k: greet(s, (p + k) % np_))

    @pl.when(q != p)
    def _():
        greet(p * ny + y, q)

    turned = filt[...].T
    for k in range(cpd):
        Fs[:, k, :] = turned[k * ns:(k + 1) * ns]
    Fr[pl.ds(s, 1)] = Fs[pl.ds(s, 1)]
    local(feat.at[:, lanes(y)], F.at[y, :, lanes(p)], loc.at[0])
    local(win, Wb.at[q], loc.at[1])

    @pl.when(q == p)
    def _():
        local(wout, Wo.at[lanes(q), lanes(y)], loc.at[2])

    pl.semaphore_wait(barrier, ns - 1 + np_ - 1 + jnp.where(q == p, 0, 1))

    def block_of(i):
        half = (i + 1) // 2
        return (y + half * (2 * (i % 2) - 1) + ny) % ny

    def spread(i):
        to = block_of(i)
        send(feat.at[:, lanes(to)], F.at[y, :, lanes(p)], sF, rF.at[y], q * ny + to, p)

    loop(1, ny, spread)
    send(win, Wb.at[q], sW, rW.at[0], far * ny + y, p)

    @pl.when(q != p)
    def _():
        send(wout, Wo.at[lanes(p), lanes(y)], sO.at[0], rO.at[0], p * ny + y, q)

    loop(1, ns, lambda k: send(Fs.at[(s + k) % ns], Fr.at[s], sV.at[0], rV.at[0], (s + k) % ns, p))

    def forward(tb):
        mine = F.at[tb, :, lanes(p)]
        for k in range(1, nzl):
            send(mine, mine, sZ, rZ.at[tb], s, ((zl + k) % nzl) * 2 + c)
        send(mine, mine, sC, rC.at[tb], s, mate)

    wait(F.at[0, :, pl.ds(0, B)], loc.at[0])
    wait(win, loc.at[1])
    forward(y)

    wait(Wb.at[0], rW.at[0])

    def weights(k):
        x = q % nx
        to = (q - x) + (x + k) % nx
        send(Wb.at[q], Wb.at[q], sW, rW.at[1], to * ny + y, p)
        send(Wb.at[far], Wb.at[far], sW, rW.at[1], to * ny + y, p)

    loop(1, nx, weights)

    def pass_on(i):
        tb = block_of(i)
        wait(F.at[0, :, pl.ds(0, B)], rF.at[tb])
        forward(tb)

    loop(1, ny, pass_on)

    @pl.when(q == p)
    def _():
        wait(wout, loc.at[2])

    @pl.when(q != p)
    def _():
        wait(wout, rO.at[0])

    own_o = Wo.at[lanes(q), lanes(y)]
    far_o = Wo.at[lanes(far), lanes(y)]
    send(own_o, own_o, sO.at[1], rO.at[1], far * ny + y, p)

    wait(Fr.at[pl.ds(0, ns - 1)], rV.at[0])
    row = lax.broadcasted_iota(jnp.int32, (B, B), 0)
    col = lax.broadcasted_iota(jnp.int32, (B, B), 1)
    causal = col >= row
    per = ns // ny

    def toeplitz(i):
        for ch in range(cpd):
            def circulant(d):
                line = jnp.broadcast_to(Fr[pl.ds(d, 1), ch, :], (B, B))
                return pltpu.roll(line, 0, 1, stride=1, stride_axis=0)

            before = circulant(jnp.maximum(i * per - 1, 0))
            before = jnp.where(i == 0, jnp.zeros_like(before), before)

            def step(j, before):
                d = i * per + j
                now = circulant(d)
                T[ch, lanes(d), :] = jnp.where(causal, now, before).astype(BF16)
                return now

            lax.fori_loop(0, per, step, before)

    def relay(tb):
        wait(F.at[0, :, pl.ds(0, (nzl - 1) * B)], rZ.at[tb])
        for k in range(1, nzl):
            other = F.at[tb, :, lanes(((zl + k) % nzl) * 2 + c)]
            send(other, other, sC, rC.at[tb], s, mate)

    def halo_to(tb):
        return q * ny + tb + 1

    @pl.when(s == 0)
    def _():
        Hr[...] = jnp.zeros_like(Hr)

    def project(tb, own):
        wait(F.at[0, :, pl.ds(0, nzl * B)], rC.at[tb])
        Ps[tb] = jnp.dot(F[tb], Wc[...], preferred_element_type=F32).astype(BF16)
        if own:
            Pr[y] = Ps[tb]
        else:
            send(Ps.at[tb], Pr.at[y], sP, rP, q * ny + tb, p)

        @pl.when(tb + 1 == y)
        def _():
            Hr[y] = Ps[tb, B - HALO:, :]

        @pl.when((tb + 1 != y) & (halo_to(tb) < ns))
        def _():
            send(Ps.at[tb, pl.ds(B - HALO, HALO), :], Hr.at[y], sH.at[tb], rH, halo_to(tb), p)

    relay(y)
    wait(Wb.at[pl.ds(0, np_ - 2)], rW.at[1])
    for k in range(np_):
        for stream in range(3):
            Wc[k * B:(k + 1) * B, stream * B:(stream + 1) * B] = Wb[k, stream]
    toeplitz(0)

    def main(i):
        relay(block_of(i))
        @pl.when(i == 1)
        def _():
            project(y, True)
        @pl.when(i > 1)
        def _():
            project(block_of(i - 1), False)
        toeplitz(i)

    loop(1, ny, main)
    project(block_of(ny - 1), False)

    wait(wout, rO.at[1])

    def along_y(k):
        to = q * ny + (y + k) % ny
        send(own_o, own_o, sO.at[2], rO.at[2], to, p)
        send(far_o, far_o, sO.at[2], rO.at[2], to, p)

    loop(1, ny, along_y)

    wait(Pr.at[pl.ds(0, ny - 1)], rP)

    @pl.when(y > 0)
    def _():
        wait(Hr.at[pl.ds(0, ny - 1)], rH)

    @pl.when((y == 0) & (q > 0))
    def _():
        wait(Hr.at[pl.ds(0, ny)], rH)

    full = Pr[0].astype(F32)
    head = Hr[0].astype(F32)
    for k in range(1, ny):
        full = full + Pr[k].astype(F32)
        head = head + Hr[k].astype(F32)
    pad[HALO:] = full.astype(BF16).astype(F32)
    pad[:HALO] = head.astype(BF16).astype(F32)
    streams = []
    for stream in range(3):
        own = slice(stream * B, (stream + 1) * B)
        total = jnp.zeros((B, B), F32)
        for j in range(3):
            total = total + taps[stream, j:j + 1, :] * pad[HALO - j:HALO - j + B, own]
        streams.append(total)
    inner = streams[1] * streams[2]
    qi[0] = streams[0]
    qi[1] = inner

    turned = inner.T
    for k in range(cpd):
        Xs[:, k, :] = turned[k * ns:(k + 1) * ns]
    Xr[pl.ds(s, 1)] = Xs[pl.ds(s, 1)]
    loop(1, ns, lambda k: send(Xs.at[(s + k) % ns], Xr.at[s], sV.at[1], rV.at[1], (s + k) % ns, p))
    Xp[:ns] = jnp.zeros((ns, B), F32)

    wait(Wo.at[pl.ds(0, 2 * B), pl.ds(0, (ny - 1) * B)], rO.at[2])

    def along_x(k):
        x = q % nx
        to = ((q - x) + (x + k) % nx) * ny + y
        send(Wo.at[lanes(q)], Wo.at[lanes(q)], sO.at[3], rO.at[3], to, p)
        send(Wo.at[lanes(far)], Wo.at[lanes(far)], sO.at[3], rO.at[3], to, p)

    loop(1, nx, along_x)

    wait(Xr.at[pl.ds(0, ns - 1)], rV.at[1])
    for ch in range(cpd):
        Xp[ns:] = Xr[:, ch, :]
        for d in range(ns):
            A[:, d * B:(d + 1) * B] = Xp[ns - d:2 * ns - d].astype(BF16)
        Ys[:, ch, :] = jnp.dot(A[...], T[ch], preferred_element_type=F32)
    Yr[pl.ds(s, 1)] = Ys[pl.ds(s, 1)]
    loop(1, ns, lambda k: send(Ys.at[(s + k) % ns], Yr.at[s], sV.at[2], rV.at[2], (s + k) % ns, p))
    wait(Yr.at[pl.ds(0, ns - 1)], rV.at[2])
    mix = jnp.concatenate([Yr[:, ch, :] for ch in range(cpd)], axis=0).T
    Gs[...] = (qi[0] * (mix + skip[...] * qi[1])).astype(BF16)

    loop(1, np_, lambda k: send(Gs, Gt.at[:, lanes(p)], sG, rG, s, (p + k) % np_))
    local(Gs, Gt.at[:, lanes(p)], loc.at[3])
    wait(Wo.at[pl.ds(0, (np_ - 2) * B)], rO.at[3])
    wait(Gs, loc.at[3])
    wait(Gt.at[:, pl.ds(0, (np_ - 1) * B)], rG)
    out[...] = jnp.dot(Gt[...], Wo[...], preferred_element_type=F32).astype(BF16)

    wait(F.at[pl.ds(0, ny - 1), :, pl.ds(0, B)], sF)
    wait(Wb.at[pl.ds(0, np_ - 1)], sW)
    wait(F.at[:, :, pl.ds(0, (nzl - 1) * B)], sZ)
    wait(F.at[:, :, pl.ds(0, nzl * B)], sC)
    wait(Pr.at[pl.ds(0, ny - 1)], sP)

    def halo_sent(tb):
        @pl.when((tb + 1 != y) & (halo_to(tb) < ns))
        def _():
            wait(Hr.at[0], sH.at[tb])

    loop(0, ny, halo_sent)
    for k in range(3):
        wait(Xs.at[pl.ds(0, ns - 1)], sV.at[k])
    wait(Gt.at[:, pl.ds(0, (np_ - 1) * B)], sG)

    @pl.when(q != p)
    def _():
        wait(wout, sO.at[0])

    wait(wout, sO.at[1])
    wait(Wo.at[pl.ds(0, 2 * B), pl.ds(0, (ny - 1) * B)], sO.at[2])
    wait(Wo.at[pl.ds(0, (np_ - 2) * B)], sO.at[3])


def per_device(features, in_proj, short_taps, long_filter, skip_gain, out_proj):
    ns, np_ = lax.axis_size("seq"), lax.axis_size("tp")
    nx = np_ // 2
    ny = ns // np_
    cpd = B // ns
    dma = pltpu.SemaphoreType.DMA
    rows = pltpu.VMEM((ns, cpd, B), F32)
    return pl.pallas_call(
        functools.partial(kernel, ny, nx),
        out_shape=jax.ShapeDtypeStruct((B, ny * B), BF16),
        in_specs=[pl.BlockSpec(memory_space=pltpu.VMEM)] * 6,
        out_specs=pl.BlockSpec(memory_space=pltpu.VMEM),
        scratch_shapes=[
            pltpu.VMEM((ny, B, np_ * B), BF16),
            pltpu.VMEM((np_, 3, B, B), BF16),
            pltpu.VMEM((np_ * B, 3 * B), BF16),
            pltpu.VMEM((ny, B, 3 * B), BF16),
            pltpu.VMEM((ny, B, 3 * B), BF16),
            pltpu.VMEM((ny, HALO, 3 * B), BF16),
            pltpu.VMEM((HALO + B, 3 * B), F32),
            pltpu.VMEM((2, B, B), F32),
            rows, rows, rows, rows, rows, rows,
            pltpu.VMEM((2 * ns, B), F32),
            pltpu.VMEM((ns, ns * B), BF16),
            pltpu.VMEM((cpd, ns * B, B), BF16),
            pltpu.VMEM((B, B), BF16),
            pltpu.VMEM((B, np_ * B), BF16),
            pltpu.VMEM((np_ * B, ny * B), BF16),
            dma((4,)),
            dma, dma((ny,)),
            dma, dma((2,)),
            dma, dma((ny,)),
            dma, dma((ny,)),
            dma, dma,
            dma((ny,)), dma,
            dma((3,)), dma((3,)),
            dma, dma,
            dma((4,)), dma((4,)),
        ],
        compiler_params=pltpu.CompilerParams(
            collective_id=0, has_side_effects=True, vmem_limit_bytes=48 * 1024 * 1024
        ),
        name="operator",
    )(features, in_proj, short_taps, long_filter, skip_gain.reshape(1, B), out_proj)


def solution(mesh):
    return jax.shard_map(
        per_device,
        mesh=mesh,
        in_specs=(
            P("seq", "tp"),
            P(None, "seq", "tp"),
            P(None, None, "tp"),
            P("seq", "tp"),
            P("tp"),
            P("tp", "seq"),
        ),
        out_specs=P("seq", "tp"),
        check_vma=False,
    )
```

time: 529 us -> 115 us (0.22)
  waiting for transfers between devices: 420 us -> 0 us
  Pallas kernels: 0 us -> 109 us
  starting transfers between devices: 65.6 us -> 0 us
  matrix products: 17.3 us -> 0 us
  between operations: 13.5 us -> 0.02 us
    all_gather x3 -> x0, waiting for transfers between devices: 274 us -> none  [the longest x1 180 us: per_device(): full_in = lax.all_gather(in_proj, 'seq', axis=1, tiled=True)]
    pallas_call x0 -> x1, Pallas kernels: none -> 109 us  [per_device(): pl.pallas_call(functools.partial(kernel, ny, nx), out_shape=jax.ShapeDtyp...]
    all_to_all x9 -> x0, waiting for transfers between devices: 91.6 us -> none  [the longest x1 13.8 us: long_convolve(): lax.all_to_all(back_imag, 'seq', split_axis=1, concat_axis=0, tiled=True)]
    all_to_all x9 -> x0, starting transfers between devices: 62.7 us -> none  [the longest x1 19.6 us: long_convolve(): lax.all_to_all(long_filter[None], 'seq', split_axis=1, concat_axis=0, til...]
    reduce_scatter x1 -> x0, waiting for transfers between devices: 51.9 us -> none  [per_device(): mixed = lax.psum_scatter(terms, 'tp', scatter_dimension=1, tiled=True)]
    dot_general x24 -> x0, matrix products: 17.3 us -> none  [the longest x22 8.34 us: contract(): jnp.einsum(form, table, values, precision=HIGHEST, preferred_element_type...]
    unnamed x6 -> x13, local copies, waits for them, and re-layouts: 0.1 us -> 5.49 us
  transfers between devices with their start and end apart: 14 -> 0, of which waited for: 12 -> 0; matrix products, arithmetic and copies ran while one was open for 4% -> 0% of each run, Pallas kernels for 0% -> 0%
where the time goes in v1:
time: 115 us; the launch traced here: 114 us
  Pallas kernels  109 us (95%)
  local copies, waits for them, and re-layouts  5.49 us (5%)
    pallas_call x1, Pallas kernels, per_device(): pl.pallas_call(functools.partial(kernel, ny, nx), out_shape=jax.ShapeDtyp...  109 us
    unnamed x13, local copies, waits for them, and re-layouts  5.49 us

profile of v1, /device:TPU:1, one launch (start us, length us, event | category | flops | bytes accessed | tf_op | source)
XLA Modules:
  0.0 114.4 jit_solution(17154850540109220931)
XLA Ops:
  0.0 0.0 copy-start.5
  0.0 0.7 copy-done.5
  0.7 0.0 copy-start
  0.7 0.9 copy-done
  1.6 0.0 copy-start.1
  1.6 0.9 copy-done.1
  2.5 0.0 copy-start.2
  2.5 0.8 copy-done.2
  3.3 0.0 copy-start.3
  3.3 0.8 copy-done.3
  4.1 0.0 copy-start.4
  4.1 0.7 copy-done.4
  4.8 108.9 %operator.1 = bf16[128,1024]{1,0:T(8,128)(2,1)S(1)} custom-call(bf16[128,1024]{1,0:T(8,128)(2,1)S(1)} %copy-done, bf16[3,128,128]{2,1,0:T(8,128)(2,1)S(1)} %copy-done.1, f32[3,3,128]{2,1,0:T(4,128)S(1)} %copy-done.4, f32[128,128]{1,0:T(8,128)S(1)} %copy-done.2, f32[1,128]{1,0:T(1,128)S(1)} %bitcast.1, bf16[128,128]{1,0:T(8,128)(2,1)S(1)} %copy-done.3), custom_call_target="tpu_custom_call" | custom-call | tf_op jit(solution)/shard_map/operator/pallas_call | solution.py:311
  113.7 0.7 copy.8
Async XLA Ops:
  0.0 0.7 copy-start.5
  0.7 0.9 copy-start
  1.6 0.9 copy-start.1
  2.5 0.8 copy-start.2
  3.3 0.8 copy-start.3
  4.1 0.7 copy-start.4

commit v2 on v1

v2 whole, which is shorter than its diff:
```python
import functools

import jax
import jax.numpy as jnp
from jax import lax
from jax.experimental import pallas as pl
from jax.experimental.pallas import tpu as pltpu
from jax.sharding import PartitionSpec as P

B = 128
HALO = 16
BF16, F32 = jnp.bfloat16, jnp.float32


def lanes(i):
    return pl.ds(pl.multiple_of(i * B, B), B)


def kernel(
    ny, nx, feat_h, win_h, taps_h, filt_h, skip_h, wout_h, out,
    feat, win, taps, filt, skip, wout,
    F, Wb, Wc, Ps, Pr, Hr, pad, qi, Fs, Fr, Xs, Xr, Ys, Yr, Xp, A, T, Gs, Gt, Wo,
    arg, loc, sF, rF, sW, rW, sZ, rZ, sE, rE, sC, rC, sP, rP, sH, rH, sV, rV, sG, rG, sO, rO,
):
    np_ = 2 * nx
    nq = 2 * nx
    nzl = np_ // 2
    ns = nq * ny
    cpd = B // ns
    s = lax.axis_index("seq")
    p = lax.axis_index("tp")
    q, y = s // ny, s % ny
    zl, c = p // 2, p % 2
    mate = p + 1 - 2 * c
    far = (q + nx) % nq
    chain = nzl == 4
    end = (zl == 0) | (zl == nzl - 1)

    def send(src, dst, ss, rs, sq, tp):
        pltpu.make_async_remote_copy(
            src_ref=src, dst_ref=dst, send_sem=ss, recv_sem=rs,
            device_id={"seq": sq, "tp": tp}, device_id_type=pl.DeviceIdType.MESH,
        ).start()

    def wait(ref, sem):
        pltpu.make_async_copy(ref, ref, sem).wait()

    def local(src, dst, sem):
        pltpu.make_async_copy(src, dst, sem).start()

    def loop(lo, hi, body):
        lax.fori_loop(lo, hi, lambda i, carry: (body(i), carry)[1], 0)

    def away(k):
        return (s + (k + ns // 3) % (ns - 1) + 1) % ns

    local(filt_h, filt, arg.at[0])
    local(feat_h, feat, arg.at[1])
    local(win_h, win, arg.at[2])
    local(wout_h, wout, arg.at[3])
    local(taps_h, taps, arg.at[4])
    local(skip_h, skip, arg.at[5])

    barrier = pltpu.get_barrier_semaphore()

    def greet(sq, tp):
        pl.semaphore_signal(
            barrier, inc=1, device_id={"seq": sq, "tp": tp}, device_id_type=pl.DeviceIdType.MESH
        )

    loop(0, ns - 1, lambda k: greet(away(k), p))
    greet(p * ny + y, far)

    @pl.when(q != p)
    def _():
        greet(p * ny + y, q)

    loop(1, np_, lambda k: greet(s, (p + k) % np_))

    wait(feat, arg.at[1])
    wait(win, arg.at[2])
    wait(wout, arg.at[3])
    local(feat.at[:, lanes(y)], F.at[y, :, lanes(p)], loc.at[0])
    local(win, Wb.at[q], loc.at[1])

    @pl.when(q == p)
    def _():
        local(wout, Wo.at[lanes(q), lanes(y)], loc.at[2])

    wait(filt, arg.at[0])
    turned = filt[...].T
    for k in range(cpd):
        Fs[:, k, :] = turned[k * ns:(k + 1) * ns]
    Fr[pl.ds(s, 1)] = Fs[pl.ds(s, 1)]
    wait(taps, arg.at[4])
    wait(skip, arg.at[5])
    wait(F.at[0, :, pl.ds(0, B)], loc.at[0])
    wait(win, loc.at[1])

    @pl.when(q == p)
    def _():
        wait(wout, loc.at[2])

    pl.semaphore_wait(barrier, ns + np_ - 1 + jnp.where(q == p, 0, 1))

    def block_of(i):
        half = jnp.where(i < 3, (i + 1) // 2, ny // 2 - (i - 2) // 2)
        sign = jnp.where(i < 3, 2 * (i % 2) - 1, 1 - 2 * (i % 2))
        return (y + half * sign + ny) % ny

    def spread(i):
        to = block_of(i)
        send(feat.at[:, lanes(to)], F.at[y, :, lanes(p)], sF, rF.at[y], q * ny + to, p)

    def forward(tb):
        mine = F.at[tb, :, lanes(p)]
        for k in range(1, nzl):
            to = (zl + k) % nzl
            if chain:
                @pl.when((to - zl != 3) & (zl - to != 3))
                def _():
                    send(mine, mine, sZ, rZ.at[tb], s, to * 2 + c)
            else:
                send(mine, mine, sZ, rZ.at[tb], s, to * 2 + c)
        send(mine, mine, sC, rC.at[tb], s, mate)

    def pass_on(i):
        tb = block_of(i)
        wait(F.at[0, :, pl.ds(0, B)], rF.at[tb])
        forward(tb)

    def blocks(n):
        return F.at[0, :, pl.ds(0, n * B)]

    def relay(tb):
        def block(z):
            return F.at[tb, :, lanes(z * 2 + c)]

        if not chain:
            wait(blocks(nzl - 1), rZ.at[tb])
            for k in range(1, nzl):
                other = block((zl + k) % nzl)
                send(other, other, sC, rC.at[tb], s, mate)
            return

        @pl.when(end)
        def _():
            wait(blocks(2), rZ.at[tb])
            for k in range(1, 3):
                other = block(jnp.where(zl == 0, k, 3 - k))
                send(other, other, sC, rC.at[tb], s, mate)

        @pl.when(jnp.logical_not(end))
        def _():
            wait(blocks(3), rZ.at[tb])
            other = block(3 * (2 - zl))
            send(other, other, sE, rE.at[tb], s, 3 * (zl - 1) * 2 + c)
            for k in range(1, 4):
                other = block((zl + k) % 4)
                send(other, other, sC, rC.at[tb], s, mate)

    def last_leg(tb):
        if not chain:
            return

        @pl.when(end)
        def _():
            wait(blocks(1), rE.at[tb])
            other = F.at[tb, :, lanes((3 - zl) * 2 + c)]
            send(other, other, sC, rC.at[tb], s, mate)

    loop(1, ny, spread)
    send(win, Wb.at[q], sW, rW.at[0], far * ny + y, p)
    forward(y)

    @pl.when(q != p)
    def _():
        send(wout, Wo.at[lanes(p), lanes(y)], sO.at[0], rO.at[0], p * ny + y, q)

    send(wout, Wo.at[lanes(p), lanes(y)], sO.at[1], rO.at[1], ((p + nx) % nq) * ny + y, q)
    loop(1, min(3, ny), pass_on)

    wait(Wb.at[0], rW.at[0])

    def weights(k):
        x = q % nx
        to = (q - x) + (x + k) % nx
        send(Wb.at[q], Wb.at[q], sW, rW.at[1], to * ny + y, p)
        send(Wb.at[far], Wb.at[far], sW, rW.at[1], to * ny + y, p)

    loop(1, nx, weights)
    loop(min(3, ny), ny, pass_on)

    @pl.when(q != p)
    def _():
        wait(wout, rO.at[0])

    wait(wout, rO.at[1])
    own_o = Wo.at[lanes(q), lanes(y)]
    far_o = Wo.at[lanes(far), lanes(y)]

    def along_y(k):
        to = q * ny + (y + k) % ny
        send(own_o, own_o, sO.at[2], rO.at[2], to, p)
        send(far_o, far_o, sO.at[2], rO.at[2], to, p)

    loop(1, ny, along_y)
    loop(0, ns - 1, lambda k: send(Fs.at[away(k)], Fr.at[s], sV.at[0], rV.at[0], away(k), p))

    row = lax.broadcasted_iota(jnp.int32, (B, B), 0)
    col = lax.broadcasted_iota(jnp.int32, (B, B), 1)
    causal = col >= row
    per = ns // 8

    def toeplitz(i):
        for ch in range(cpd):
            def circulant(d):
                line = jnp.broadcast_to(Fr[pl.ds(d, 1), ch, :], (B, B))
                return pltpu.roll(line, 0, 1, stride=1, stride_axis=0)

            before = circulant(jnp.maximum(i * per - 1, 0))
            before = jnp.where(i == 0, jnp.zeros_like(before), before)

            def step(j, before):
                d = i * per + j
                now = circulant(d)
                T[ch, lanes(d), :] = jnp.where(causal, now, before).astype(BF16)
                return now

            lax.fori_loop(0, per, step, before)

    def halo_to(tb):
        return q * ny + tb + 1

    @pl.when(s == 0)
    def _():
        Hr[...] = jnp.zeros_like(Hr)

    def project(tb, own):
        wait(blocks(nzl), rC.at[tb])
        Ps[tb] = jnp.dot(F[tb], Wc[...], preferred_element_type=F32).astype(BF16)
        if own:
            Pr[y] = Ps[tb]
        else:
            send(Ps.at[tb], Pr.at[y], sP, rP, q * ny + tb, p)

        @pl.when(tb + 1 == y)
        def _():
            Hr[y] = Ps[tb, B - HALO:, :]

        @pl.when((tb + 1 != y) & (halo_to(tb) < ns))
        def _():
            send(Ps.at[tb, pl.ds(B - HALO, HALO), :], Hr.at[y], sH.at[tb], rH, halo_to(tb), p)

    relay(y)
    wait(Wb.at[pl.ds(0, np_ - 2)], rW.at[1])
    for k in range(np_):
        for stream in range(3):
            Wc[k * B:(k + 1) * B, stream * B:(stream + 1) * B] = Wb[k, stream]

    def along_x(k):
        x = q % nx
        to = ((q - x) + (x + k) % nx) * ny + y
        send(Wo.at[lanes(q)], Wo.at[lanes(q)], sO.at[3], rO.at[3], to, p)
        send(Wo.at[lanes(far)], Wo.at[lanes(far)], sO.at[3], rO.at[3], to, p)

    def main(i):
        relay(block_of(i))
        last_leg(block_of(i - 1))

        @pl.when(i == 2)
        def _():
            project(y, True)

        @pl.when(i > 2)
        def _():
            project(block_of(i - 2), False)

        @pl.when(i == min(3, ny - 1))
        def _():
            wait(Wo.at[pl.ds(0, 2 * B), pl.ds(0, (ny - 1) * B)], rO.at[2])
            loop(1, nx, along_x)
            wait(Fr.at[pl.ds(0, ns - 1)], rV.at[0])

        @pl.when(i >= 4)
        def _():
            toeplitz(i - 4)

    loop(1, ny, main)
    last_leg(block_of(ny - 1))
    if ny > 2:
        project(block_of(ny - 2), False)
    else:
        project(y, True)
    project(block_of(ny - 1), False)
    loop(max(ny - 4, 0), 6, toeplitz)

    wait(Pr.at[pl.ds(0, ny - 1)], rP)

    @pl.when(y > 0)
    def _():
        wait(Hr.at[pl.ds(0, ny - 1)], rH)

    @pl.when((y == 0) & (q > 0))
    def _():
        wait(Hr.at[pl.ds(0, ny)], rH)

    full = Pr[0].astype(F32)
    head = Hr[0].astype(F32)
    for k in range(1, ny):
        full = full + Pr[k].astype(F32)
        head = head + Hr[k].astype(F32)
    pad[HALO:] = full
    pad[:HALO] = head
    streams = []
    for stream in range(3):
        own = slice(stream * B, (stream + 1) * B)
        total = jnp.zeros((B, B), F32)
        for j in range(3):
            total = total + taps[stream, j:j + 1, :] * pad[HALO - j:HALO - j + B, own]
        streams.append(total)
    inner = streams[1] * streams[2]
    qi[0] = streams[0]
    qi[1] = inner

    turned = inner.T
    for k in range(cpd):
        Xs[:, k, :] = turned[k * ns:(k + 1) * ns]
    Xr[pl.ds(s, 1)] = Xs[pl.ds(s, 1)]
    loop(0, ns - 1, lambda k: send(Xs.at[away(k)], Xr.at[s], sV.at[1], rV.at[1], away(k), p))
    Xp[:ns] = jnp.zeros((ns, B), F32)
    loop(6, 8, toeplitz)

    wait(Xr.at[pl.ds(0, ns - 1)], rV.at[1])
    for ch in range(cpd):
        Xp[ns:] = Xr[:, ch, :]
        for d in range(ns):
            A[:, d * B:(d + 1) * B] = Xp[ns - d:2 * ns - d].astype(BF16)
        Ys[:, ch, :] = jnp.dot(A[...], T[ch], preferred_element_type=F32)
    Yr[pl.ds(s, 1)] = Ys[pl.ds(s, 1)]
    loop(0, ns - 1, lambda k: send(Ys.at[away(k)], Yr.at[s], sV.at[2], rV.at[2], away(k), p))
    wait(Yr.at[pl.ds(0, ns - 1)], rV.at[2])
    mix = jnp.concatenate([Yr[:, ch, :] for ch in range(cpd)], axis=0).T
    Gs[...] = (qi[0] * (mix + skip[...] * qi[1])).astype(BF16)

    gated = Gt.at[:, lanes(p)]
    for k in range(1, nzl):
        send(Gs, gated, sG, rG.at[0], s, ((zl + k) % nzl) * 2 + c)
    send(Gs, gated, sG, rG.at[1], s, mate)
    local(Gs, gated, loc.at[0])
    wait(Wo.at[pl.ds(0, (np_ - 2) * B)], rO.at[3])
    wait(Gs, loc.at[0])
    wait(Gt.at[:, pl.ds(0, (nzl - 1) * B)], rG.at[0])
    for k in range(1, nzl):
        other = Gt.at[:, lanes(((zl + k) % nzl) * 2 + c)]
        send(other, other, sG, rG.at[1], s, mate)
    wait(Gt.at[:, pl.ds(0, nzl * B)], rG.at[1])
    out[...] = jnp.dot(Gt[...], Wo[...], preferred_element_type=F32).astype(BF16)

    wait(F.at[pl.ds(0, ny - 1), :, pl.ds(0, B)], sF)
    wait(Wb.at[pl.ds(0, np_ - 1)], sW)
    if chain:
        @pl.when(end)
        def _():
            wait(F.at[:, :, pl.ds(0, 2 * B)], sZ)

        @pl.when(jnp.logical_not(end))
        def _():
            wait(F.at[:, :, pl.ds(0, 3 * B)], sZ)
            wait(F.at[:, :, pl.ds(0, B)], sE)
    else:
        wait(F.at[:, :, pl.ds(0, (nzl - 1) * B)], sZ)
    wait(F.at[:, :, pl.ds(0, nzl * B)], sC)
    wait(Pr.at[pl.ds(0, ny - 1)], sP)

    def halo_sent(tb):
        @pl.when((tb + 1 != y) & (halo_to(tb) < ns))
        def _():
            wait(Hr.at[0], sH.at[tb])

    loop(0, ny, halo_sent)
    for k in range(3):
        wait(Xs.at[pl.ds(0, ns - 1)], sV.at[k])
    wait(Gt.at[:, pl.ds(0, (2 * nzl - 1) * B)], sG)

    @pl.when(q != p)
    def _():
        wait(wout, sO.at[0])

    wait(wout, sO.at[1])
    wait(Wo.at[pl.ds(0, 2 * B), pl.ds(0, (ny - 1) * B)], sO.at[2])
    wait(Wo.at[pl.ds(0, (np_ - 2) * B)], sO.at[3])


def per_device(features, in_proj, short_taps, long_filter, skip_gain, out_proj):
    ns, np_ = lax.axis_size("seq"), lax.axis_size("tp")
    nx = np_ // 2
    ny = ns // np_
    cpd = B // ns
    dma = pltpu.SemaphoreType.DMA
    rows = pltpu.VMEM((ns, cpd, B), F32)
    return pl.pallas_call(
        functools.partial(kernel, ny, nx),
        out_shape=jax.ShapeDtypeStruct((B, ny * B), BF16),
        in_specs=[pl.BlockSpec(memory_space=pl.ANY)] * 6,
        out_specs=pl.BlockSpec(memory_space=pltpu.VMEM),
        scratch_shapes=[
            pltpu.VMEM((B, ny * B), BF16),
            pltpu.VMEM((3, B, B), BF16),
            pltpu.VMEM((3, 3, B), F32),
            pltpu.VMEM((B, B), F32),
            pltpu.VMEM((1, B), F32),
            pltpu.VMEM((B, B), BF16),
            pltpu.VMEM((ny, B, np_ * B), BF16),
            pltpu.VMEM((np_, 3, B, B), BF16),
            pltpu.VMEM((np_ * B, 3 * B), BF16),
            pltpu.VMEM((ny, B, 3 * B), BF16),
            pltpu.VMEM((ny, B, 3 * B), BF16),
            pltpu.VMEM((ny, HALO, 3 * B), BF16),
            pltpu.VMEM((HALO + B, 3 * B), F32),
            pltpu.VMEM((2, B, B), F32),
            rows, rows, rows, rows, rows, rows,
            pltpu.VMEM((2 * ns, B), F32),
            pltpu.VMEM((ns, ns * B), BF16),
            pltpu.VMEM((cpd, ns * B, B), BF16),
            pltpu.VMEM((B, B), BF16),
            pltpu.VMEM((B, np_ * B), BF16),
            pltpu.VMEM((np_ * B, ny * B), BF16),
            dma((6,)), dma((3,)),
            dma, dma((ny,)),
            dma, dma((2,)),
            dma, dma((ny,)),
            dma, dma((ny,)),
            dma, dma((ny,)),
            dma, dma,
            dma((ny,)), dma,
            dma((3,)), dma((3,)),
            dma, dma((2,)),
            dma((4,)), dma((4,)),
        ],
        compiler_params=pltpu.CompilerParams(
            collective_id=0, has_side_effects=True
        ),
        name="operator",
    )(features, in_proj, short_taps, long_filter, skip_gain.reshape(1, B), out_proj)


def solution(mesh):
    return jax.shard_map(
        per_device,
        mesh=mesh,
        in_specs=(
            P("seq", "tp"),
            P(None, "seq", "tp"),
            P(None, None, "tp"),
            P("seq", "tp"),
            P("tp"),
            P("tp", "seq"),
        ),
        out_specs=P("seq", "tp"),
        check_vma=False,
    )
```

time: 115 us -> 102 us (0.89)
  Pallas kernels: 109 us -> 100 us
  local copies, waits for them, and re-layouts: 5.49 us -> 1.67 us
    pallas_call x1, Pallas kernels: 109 us -> 100 us  [per_device(): pl.pallas_call(functools.partial(kernel, ny, nx), out_shape=jax.ShapeDtyp...]
    unnamed x13 -> x1, local copies, waits for them, and re-layouts: 5.49 us -> 1.67 us
where the time goes in v2:
time: 102 us
  Pallas kernels  100 us (98%)
  local copies, waits for them, and re-layouts  1.67 us (2%)
    pallas_call x1, Pallas kernels, per_device(): pl.pallas_call(functools.partial(kernel, ny, nx), out_shape=jax.ShapeDtyp...  100 us

profile of v2, /device:TPU:1, one launch (start us, length us, event | category | flops | bytes accessed | tf_op | source)
XLA Modules:
  0.0 101.8 jit_solution(5718455964447475152)
XLA Ops:
  0.0 100.1 %operator.1 = bf16[128,1024]{1,0:T(8,128)(2,1)} custom-call(bf16[128,1024]{1,0:T(8,128)(2,1)} %feat_h.1, bf16[3,128,128]{2,1,0:T(8,128)(2,1)} %win_h.1, f32[3,3,128]{2,1,0:T(4,128)} %taps_h.1, f32[128,128]{1,0:T(8,128)} %filt_h.1, f32[1,128]{1,0:T(1,128)} %bitcast.1, bf16[128,128]{1,0:T(8,128)(2,1)} %wout_h.1), custom_call_target="tpu_custom_call" | custom-call | tf_op jit(solution)/shard_map/operator/pallas_call | solution.py:402
  100.2 1.7 %copy.8 = bf16[128,1024]{1,0:T(8,128)(2,1)} copy(bf16[128,1024]{1,0:T(8,128)(2,1)} %operator.1) | data formatting | bytes 524288

commit v3 on v2

--- a/solution.py
+++ b/solution.py
@@ -20,7 +20,7 @@
     ny, nx, feat_h, win_h, taps_h, filt_h, skip_h, wout_h, out,
     feat, win, taps, filt, skip, wout,
     F, Wb, Wc, Ps, Pr, Hr, pad, qi, Fs, Fr, Xs, Xr, Ys, Yr, Xp, A, T, Gs, Gt, Wo,
-    arg, loc, sF, rF, sW, rW, sZ, rZ, sE, rE, sC, rC, sP, rP, sH, rH, sV, rV, sG, rG, sO, rO,
+    arg, loc, sF, rF, sW, rW, sZ, rZ, sE, rE, sC, rC, sP, rP, sH, rH, sV, rV, sG, rG, sO, rO, rU, rD,
 ):
     np_ = 2 * nx
     nq = 2 * nx
@@ -173,38 +173,68 @@
     send(win, Wb.at[q], sW, rW.at[0], far * ny + y, p)
     forward(y)
 
+    def weights(which, sem):
+        def step(k):
+            x = q % nx
+            to = (q - x) + (x + k) % nx
+            send(Wb.at[which], Wb.at[which], sW, sem, to * ny + y, p)
+
+        loop(1, nx, step)
+
+    weights(q, rW.at[1])
+
     @pl.when(q != p)
     def _():
         send(wout, Wo.at[lanes(p), lanes(y)], sO.at[0], rO.at[0], p * ny + y, q)
 
     send(wout, Wo.at[lanes(p), lanes(y)], sO.at[1], rO.at[1], ((p + nx) % nq) * ny + y, q)
-    loop(1, min(3, ny), pass_on)
-
+    loop(1, ny, pass_on)
     wait(Wb.at[0], rW.at[0])
-
-    def weights(k):
-        x = q % nx
-        to = (q - x) + (x + k) % nx
-        send(Wb.at[q], Wb.at[q], sW, rW.at[1], to * ny + y, p)
-        send(Wb.at[far], Wb.at[far], sW, rW.at[1], to * ny + y, p)
-
-    loop(1, nx, weights)
-    loop(min(3, ny), ny, pass_on)
+    weights(far, rW.at[2])
 
     @pl.when(q != p)
     def _():
         wait(wout, rO.at[0])
 
     wait(wout, rO.at[1])
-    own_o = Wo.at[lanes(q), lanes(y)]
-    far_o = Wo.at[lanes(far), lanes(y)]
-
-    def along_y(k):
-        to = q * ny + (y + k) % ny
-        send(own_o, own_o, sO.at[2], rO.at[2], to, p)
-        send(far_o, far_o, sO.at[2], rO.at[2], to, p)
-
-    loop(1, ny, along_y)
+    reach = ny // 2
+    x_pos = q % nx
+    right = ((q - x_pos) + (x_pos + 1) % nx) * ny + y
+    left = ((q - x_pos) + (x_pos + nx - 1) % nx) * ny + y
+
+    def near(k):
+        return q * ny + (y + k + ny) % ny
+
+    def piece(rows, k):
+        return Wo.at[lanes(rows), lanes((y + k + ny) % ny)]
+
+    def sideways(block):
+        send(block, block, sO.at[3], rO.at[3], right, p)
+        if nx > 2:
+            send(block, block, sO.at[4], rO.at[4], left, p)
+
+    def ring(t):
+        if t > 0:
+            wait(wout, rU.at[t - 1])
+            wait(wout, rD.at[t - 1])
+            sideways(piece(q, -t))
+            sideways(piece(far, t))
+            if t < reach:
+                wait(wout, rU.at[reach + t - 1])
+                wait(wout, rD.at[reach + t - 1])
+                sideways(piece(far, -t))
+                sideways(piece(q, t))
+        else:
+            sideways(piece(q, 0))
+            sideways(piece(far, 0))
+        if t < reach:
+            send(piece(q, -t), piece(q, -t), sO.at[2], rU.at[t], near(1), p)
+            send(piece(far, t), piece(far, t), sO.at[2], rD.at[t], near(-1), p)
+        if t < reach - 1:
+            send(piece(far, -t), piece(far, -t), sO.at[2], rU.at[reach + t], near(1), p)
+            send(piece(q, t), piece(q, t), sO.at[2], rD.at[reach + t], near(-1), p)
+
+    ring(0)
     loop(0, ns - 1, lambda k: send(Fs.at[away(k)], Fr.at[s], sV.at[0], rV.at[0], away(k), p))
 
     row = lax.broadcasted_iota(jnp.int32, (B, B), 0)
@@ -215,8 +245,10 @@
     def toeplitz(i):
         for ch in range(cpd):
             def circulant(d):
-                line = jnp.broadcast_to(Fr[pl.ds(d, 1), ch, :], (B, B))
-                return pltpu.roll(line, 0, 1, stride=1, stride_axis=0)
+                line = jnp.broadcast_to(Fr[pl.ds(d, 1), ch, :], (8, B))
+                first = pltpu.roll(line, 0, 1, stride=1, stride_axis=0)
+                rest = [pltpu.roll(first, 8 * k, 1) for k in range(1, B // 8)]
+                return jnp.concatenate([first] + rest, axis=0)
 
             before = circulant(jnp.maximum(i * per - 1, 0))
             before = jnp.where(i == 0, jnp.zeros_like(before), before)
@@ -253,17 +285,14 @@
             send(Ps.at[tb, pl.ds(B - HALO, HALO), :], Hr.at[y], sH.at[tb], rH, halo_to(tb), p)
 
     relay(y)
-    wait(Wb.at[pl.ds(0, np_ - 2)], rW.at[1])
+    if reach > 1:
+        ring(1)
+    wait(Wb.at[pl.ds(0, nx - 1)], rW.at[1])
+    wait(Wb.at[pl.ds(0, nx - 1)], rW.at[2])
     for k in range(np_):
         for stream in range(3):
             Wc[k * B:(k + 1) * B, stream * B:(stream + 1) * B] = Wb[k, stream]
 
-    def along_x(k):
-        x = q % nx
-        to = ((q - x) + (x + k) % nx) * ny + y
-        send(Wo.at[lanes(q)], Wo.at[lanes(q)], sO.at[3], rO.at[3], to, p)
-        send(Wo.at[lanes(far)], Wo.at[lanes(far)], sO.at[3], rO.at[3], to, p)
-
     def main(i):
         relay(block_of(i))
         last_leg(block_of(i - 1))
@@ -276,16 +305,13 @@
         def _():
             project(block_of(i - 2), False)
 
-        @pl.when(i == min(3, ny - 1))
-        def _():
-            wait(Wo.at[pl.ds(0, 2 * B), pl.ds(0, (ny - 1) * B)], rO.at[2])
-            loop(1, nx, along_x)
-            wait(Fr.at[pl.ds(0, ns - 1)], rV.at[0])
-
-        @pl.when(i >= 4)
-        def _():
-            toeplitz(i - 4)
-
+        for t in range(2, reach + 1):
+            @pl.when(i == t - 1)
+            def _(t=t):
+                ring(t)
+
+    if reach == 1:
+        ring(1)
     loop(1, ny, main)
     last_leg(block_of(ny - 1))
     if ny > 2:
@@ -293,7 +319,17 @@
     else:
         project(y, True)
     project(block_of(ny - 1), False)
-    loop(max(ny - 4, 0), 6, toeplitz)
+
+    sides = Wo.at[pl.ds(0, 2 * B)]
+    wait(sides, rO.at[3])
+    if nx > 2:
+        wait(sides, rO.at[4])
+        below = (q - x_pos) + (x_pos + nx - 1) % nx
+        above = (far - x_pos % nx) + (x_pos + 1) % nx
+        send(Wo.at[lanes(below)], Wo.at[lanes(below)], sO.at[5], rO.at[5], right, p)
+        send(Wo.at[lanes(above)], Wo.at[lanes(above)], sO.at[5], rO.at[5], left, p)
+    wait(Fr.at[pl.ds(0, ns - 1)], rV.at[0])
+    loop(0, 6, toeplitz)
 
     wait(Pr.at[pl.ds(0, ny - 1)], rP)
 
@@ -348,7 +384,8 @@
         send(Gs, gated, sG, rG.at[0], s, ((zl + k) % nzl) * 2 + c)
     send(Gs, gated, sG, rG.at[1], s, mate)
     local(Gs, gated, loc.at[0])
-    wait(Wo.at[pl.ds(0, (np_ - 2) * B)], rO.at[3])
+    if nx > 2:
+        wait(sides, rO.at[5])
     wait(Gs, loc.at[0])
     wait(Gt.at[:, pl.ds(0, (nzl - 1) * B)], rG.at[0])
     for k in range(1, nzl):
@@ -389,7 +426,10 @@
 
     wait(wout, sO.at[1])
     wait(Wo.at[pl.ds(0, 2 * B), pl.ds(0, (ny - 1) * B)], sO.at[2])
-    wait(Wo.at[pl.ds(0, (np_ - 2) * B)], sO.at[3])
+    wait(sides, sO.at[3])
+    if nx > 2:
+        wait(sides, sO.at[4])
+        wait(sides, sO.at[5])
 
 
 def per_device(features, in_proj, short_taps, long_filter, skip_gain, out_proj):
@@ -428,7 +468,7 @@
             pltpu.VMEM((np_ * B, ny * B), BF16),
             dma((6,)), dma((3,)),
             dma, dma((ny,)),
-            dma, dma((2,)),
+            dma, dma((3,)),
             dma, dma((ny,)),
             dma, dma((ny,)),
             dma, dma((ny,)),
@@ -436,7 +476,7 @@
             dma((ny,)), dma,
             dma((3,)), dma((3,)),
             dma, dma((2,)),
-            dma((4,)), dma((4,)),
+            dma((6,)), dma((6,)), dma((ny,)), dma((ny,)),
         ],
         compiler_params=pltpu.CompilerParams(
             collective_id=0, has_side_effects=True

time: 102 us -> 98.5 us (0.966)
  Pallas kernels: 100 us -> 96.7 us
    pallas_call x1, Pallas kernels: 100 us -> 96.7 us  [per_device(): pl.pallas_call(functools.partial(kernel, ny, nx), out_shape=jax.ShapeDtyp...]
where the time goes in v3:
time: 98.5 us; the launch traced here: 98.4 us
  Pallas kernels  96.7 us (98%)
  local copies, waits for them, and re-layouts  1.67 us (2%)
    pallas_call x1, Pallas kernels, per_device(): pl.pallas_call(functools.partial(kernel, ny, nx), out_shape=jax.ShapeDtyp...  96.7 us

profile of v3, /device:TPU:1, one launch (start us, length us, event | category | flops | bytes accessed | tf_op | source)
XLA Modules:
  0.0 98.4 jit_solution(17280728410467352453)
XLA Ops:
  0.0 96.7 %operator.1 = bf16[128,1024]{1,0:T(8,128)(2,1)} custom-call(bf16[128,1024]{1,0:T(8,128)(2,1)} %feat_h.1, bf16[3,128,128]{2,1,0:T(8,128)(2,1)} %win_h.1, f32[3,3,128]{2,1,0:T(4,128)} %taps_h.1, f32[128,128]{1,0:T(8,128)} %filt_h.1, f32[1,128]{1,0:T(1,128)} %bitcast.1, bf16[128,128]{1,0:T(8,128)(2,1)} %wout_h.1), custom_call_target="tpu_custom_call" | custom-call | tf_op jit(solution)/shard_map/operator/pallas_call | solution.py:442
  96.7 1.7 %copy.8 = bf16[128,1024]{1,0:T(8,128)(2,1)} copy(bf16[128,1024]{1,0:T(8,128)(2,1)} %operator.1) | data formatting | bytes 524288

commit v4 on v3

--- a/solution.py
+++ b/solution.py
@@ -19,8 +19,8 @@
 def kernel(
     ny, nx, feat_h, win_h, taps_h, filt_h, skip_h, wout_h, out,
     feat, win, taps, filt, skip, wout,
-    F, Wb, Wc, Ps, Pr, Hr, pad, qi, Fs, Fr, Xs, Xr, Ys, Yr, Xp, A, T, Gs, Gt, Wo,
-    arg, loc, sF, rF, sW, rW, sZ, rZ, sE, rE, sC, rC, sP, rP, sH, rH, sV, rV, sG, rG, sO, rO, rU, rD,
+    F, Wb, Wc, Ps, Pr, Pf, Pe, Hs, Hr, pad, qi, Fs, Fr, Xs, Xr, Ys, Yr, Xp, A, T, Gs, Gt, Wo,
+    arg, loc, sF, rF, sW, rW, sZ, rZ, sE, rE, sC, rC, sP, rP, rN, sH, rH, sV, rV, sG, rG, sO, rO, rU, rD, rR, rL,
 ):
     np_ = 2 * nx
     nq = 2 * nx
@@ -103,10 +103,16 @@
 
     pl.semaphore_wait(barrier, ns + np_ - 1 + jnp.where(q == p, 0, 1))
 
+    reach = ny // 2
+
+    def distance(i):
+        return reach - i // 2 if i % 2 == 0 else i // 2 + 1 - reach
+
+    def near(k):
+        return q * ny + (y + k + ny) % ny
+
     def block_of(i):
-        half = jnp.where(i < 3, (i + 1) // 2, ny // 2 - (i - 2) // 2)
-        sign = jnp.where(i < 3, 2 * (i % 2) - 1, 1 - 2 * (i % 2))
-        return (y + half * sign + ny) % ny
+        return (y + distance(i) + ny) % ny
 
     def spread(i):
         to = block_of(i)
@@ -169,7 +175,8 @@
             other = F.at[tb, :, lanes((3 - zl) * 2 + c)]
             send(other, other, sC, rC.at[tb], s, mate)
 
-    loop(1, ny, spread)
+    for i in range(ny - 1):
+        spread(i)
     send(win, Wb.at[q], sW, rW.at[0], far * ny + y, p)
     forward(y)
 
@@ -188,7 +195,8 @@
         send(wout, Wo.at[lanes(p), lanes(y)], sO.at[0], rO.at[0], p * ny + y, q)
 
     send(wout, Wo.at[lanes(p), lanes(y)], sO.at[1], rO.at[1], ((p + nx) % nq) * ny + y, q)
-    loop(1, ny, pass_on)
+    for i in range(ny - 1):
+        pass_on(i)
     wait(Wb.at[0], rW.at[0])
     weights(far, rW.at[2])
 
@@ -197,36 +205,46 @@
         wait(wout, rO.at[0])
 
     wait(wout, rO.at[1])
-    reach = ny // 2
     x_pos = q % nx
     right = ((q - x_pos) + (x_pos + 1) % nx) * ny + y
     left = ((q - x_pos) + (x_pos + nx - 1) % nx) * ny + y
 
-    def near(k):
-        return q * ny + (y + k + ny) % ny
-
     def piece(rows, k):
         return Wo.at[lanes(rows), lanes((y + k + ny) % ny)]
 
-    def sideways(block):
-        send(block, block, sO.at[3], rO.at[3], right, p)
+    def sideways(block, t):
+        send(block, block, sO.at[3], rR.at[t], right, p)
         if nx > 2:
-            send(block, block, sO.at[4], rO.at[4], left, p)
+            send(block, block, sO.at[4], rL.at[t], left, p)
+
+    def columns(t):
+        return (0,) if t == 0 else (t,) if t == reach else (-t, t)
+
+    def across(t):
+        got = Wo.at[pl.ds(0, B), pl.ds(0, 2 * len(columns(t)) * B)]
+        wait(got, rR.at[t])
+        if nx > 2:
+            wait(got, rL.at[t])
+            below = (q - x_pos) + (x_pos + nx - 1) % nx
+            above = (far - x_pos) + (x_pos + 1) % nx
+            for k in columns(t):
+                send(piece(below, k), piece(below, k), sO.at[5], rO.at[5], right, p)
+                send(piece(above, k), piece(above, k), sO.at[5], rO.at[5], left, p)
 
     def ring(t):
         if t > 0:
             wait(wout, rU.at[t - 1])
             wait(wout, rD.at[t - 1])
-            sideways(piece(q, -t))
-            sideways(piece(far, t))
+            sideways(piece(q, -t), t)
+            sideways(piece(far, t), t)
             if t < reach:
                 wait(wout, rU.at[reach + t - 1])
                 wait(wout, rD.at[reach + t - 1])
-                sideways(piece(far, -t))
-                sideways(piece(q, t))
+                sideways(piece(far, -t), t)
+                sideways(piece(q, t), t)
         else:
-            sideways(piece(q, 0))
-            sideways(piece(far, 0))
+            sideways(piece(q, 0), 0)
+            sideways(piece(far, 0), 0)
         if t < reach:
             send(piece(q, -t), piece(q, -t), sO.at[2], rU.at[t], near(1), p)
             send(piece(far, t), piece(far, t), sO.at[2], rD.at[t], near(-1), p)
@@ -245,10 +263,8 @@
     def toeplitz(i):
         for ch in range(cpd):
             def circulant(d):
-                line = jnp.broadcast_to(Fr[pl.ds(d, 1), ch, :], (8, B))
-                first = pltpu.roll(line, 0, 1, stride=1, stride_axis=0)
-                rest = [pltpu.roll(first, 8 * k, 1) for k in range(1, B // 8)]
-                return jnp.concatenate([first] + rest, axis=0)
+                line = jnp.broadcast_to(Fr[pl.ds(d, 1), ch, :], (B, B))
+                return pltpu.roll(line, 0, 1, stride=1, stride_axis=0)
 
             before = circulant(jnp.maximum(i * per - 1, 0))
             before = jnp.where(i == 0, jnp.zeros_like(before), before)
@@ -259,7 +275,7 @@
                 T[ch, lanes(d), :] = jnp.where(causal, now, before).astype(BF16)
                 return now
 
-            lax.fori_loop(0, per, step, before)
+            lax.fori_loop(0, per, step, before, unroll=True)
 
     def halo_to(tb):
         return q * ny + tb + 1
@@ -268,70 +284,67 @@
     def _():
         Hr[...] = jnp.zeros_like(Hr)
 
-    def project(tb, own):
+    def project(i):
+        k, tb = distance(i), block_of(i)
         wait(blocks(nzl), rC.at[tb])
-        Ps[tb] = jnp.dot(F[tb], Wc[...], preferred_element_type=F32).astype(BF16)
-        if own:
-            Pr[y] = Ps[tb]
+        total = jnp.dot(F[tb], Wc[...], preferred_element_type=F32)
+        Hs[i] = total[B - HALO:].astype(BF16)
+
+        @pl.when(tb + 1 == y)
+        def _():
+            Hr[y] = Hs[i]
+
+        @pl.when((tb + 1 != y) & (halo_to(tb) < ns))
+        def _():
+            send(Hs.at[i], Hr.at[y], sH.at[i], rH, halo_to(tb), p)
+
+        side = 0 if k > 0 else 1
+        if k == 0:
+            pad[HALO:] = total
+            return
+        if abs(k) < reach - side:
+            wait(Ps.at[0], rP.at[i])
+            total = total + Pr[i].astype(F32)
+        to = near(1 - 2 * side)
+        if abs(k) == 1:
+            Pf[side] = total
+            send(Pf.at[side], Pe.at[side], sP.at[i], rN.at[side], to, p)
         else:
-            send(Ps.at[tb], Pr.at[y], sP, rP, q * ny + tb, p)
-
-        @pl.when(tb + 1 == y)
-        def _():
-            Hr[y] = Ps[tb, B - HALO:, :]
-
-        @pl.when((tb + 1 != y) & (halo_to(tb) < ns))
-        def _():
-            send(Ps.at[tb, pl.ds(B - HALO, HALO), :], Hr.at[y], sH.at[tb], rH, halo_to(tb), p)
+            Ps[i] = total.astype(BF16)
+            send(Ps.at[i], Pr.at[i + 2], sP.at[i], rP.at[i + 2], to, p)
 
     relay(y)
-    if reach > 1:
-        ring(1)
     wait(Wb.at[pl.ds(0, nx - 1)], rW.at[1])
     wait(Wb.at[pl.ds(0, nx - 1)], rW.at[2])
     for k in range(np_):
         for stream in range(3):
             Wc[k * B:(k + 1) * B, stream * B:(stream + 1) * B] = Wb[k, stream]
 
-    def main(i):
+    last_leg(y)
+    for i in range(ny - 1):
         relay(block_of(i))
-        last_leg(block_of(i - 1))
-
-        @pl.when(i == 2)
-        def _():
-            project(y, True)
-
-        @pl.when(i > 2)
-        def _():
-            project(block_of(i - 2), False)
-
-        for t in range(2, reach + 1):
-            @pl.when(i == t - 1)
-            def _(t=t):
-                ring(t)
-
-    if reach == 1:
-        ring(1)
-    loop(1, ny, main)
-    last_leg(block_of(ny - 1))
+        if i >= 1:
+            last_leg(block_of(i - 1))
+        if i >= 2:
+            project(i - 2)
+        if i % 2 == 1 and i // 2 + 1 <= reach:
+            ring(i // 2 + 1)
+            across(i // 2)
+    last_leg(block_of(ny - 2))
     if ny > 2:
-        project(block_of(ny - 2), False)
-    else:
-        project(y, True)
-    project(block_of(ny - 1), False)
-
-    sides = Wo.at[pl.ds(0, 2 * B)]
-    wait(sides, rO.at[3])
-    if nx > 2:
-        wait(sides, rO.at[4])
-        below = (q - x_pos) + (x_pos + nx - 1) % nx
-        above = (far - x_pos % nx) + (x_pos + 1) % nx
-        send(Wo.at[lanes(below)], Wo.at[lanes(below)], sO.at[5], rO.at[5], right, p)
-        send(Wo.at[lanes(above)], Wo.at[lanes(above)], sO.at[5], rO.at[5], left, p)
+        project(ny - 3)
+    project(ny - 2)
+    ring(reach)
+    across(reach - 1)
+    project(ny - 1)
     wait(Fr.at[pl.ds(0, ns - 1)], rV.at[0])
-    loop(0, 6, toeplitz)
-
-    wait(Pr.at[pl.ds(0, ny - 1)], rP)
+    loop(0, 8, toeplitz)
+    across(reach)
+
+    full = pad[HALO:]
+    for side in range(2 if ny > 2 else 1):
+        wait(Pe.at[0], rN.at[side])
+        full = full + Pe[side]
 
     @pl.when(y > 0)
     def _():
@@ -341,10 +354,8 @@
     def _():
         wait(Hr.at[pl.ds(0, ny)], rH)
 
-    full = Pr[0].astype(F32)
     head = Hr[0].astype(F32)
     for k in range(1, ny):
-        full = full + Pr[k].astype(F32)
         head = head + Hr[k].astype(F32)
     pad[HALO:] = full
     pad[:HALO] = head
@@ -365,7 +376,6 @@
     Xr[pl.ds(s, 1)] = Xs[pl.ds(s, 1)]
     loop(0, ns - 1, lambda k: send(Xs.at[away(k)], Xr.at[s], sV.at[1], rV.at[1], away(k), p))
     Xp[:ns] = jnp.zeros((ns, B), F32)
-    loop(6, 8, toeplitz)
 
     wait(Xr.at[pl.ds(0, ns - 1)], rV.at[1])
     for ch in range(cpd):
@@ -385,7 +395,7 @@
     send(Gs, gated, sG, rG.at[1], s, mate)
     local(Gs, gated, loc.at[0])
     if nx > 2:
-        wait(sides, rO.at[5])
+        wait(Wo.at[pl.ds(0, 2 * B)], rO.at[5])
     wait(Gs, loc.at[0])
     wait(Gt.at[:, pl.ds(0, (nzl - 1) * B)], rG.at[0])
     for k in range(1, nzl):
@@ -408,14 +418,16 @@
     else:
         wait(F.at[:, :, pl.ds(0, (nzl - 1) * B)], sZ)
     wait(F.at[:, :, pl.ds(0, nzl * B)], sC)
-    wait(Pr.at[pl.ds(0, ny - 1)], sP)
-
-    def halo_sent(tb):
+    for i in range(ny):
+        tb = block_of(i)
+
         @pl.when((tb + 1 != y) & (halo_to(tb) < ns))
-        def _():
-            wait(Hr.at[0], sH.at[tb])
-
-    loop(0, ny, halo_sent)
+        def _(i=i):
+            wait(Hr.at[0], sH.at[i])
+
+        if distance(i) != 0:
+            wait(Pe.at[0] if abs(distance(i)) == 1 else Ps.at[0], sP.at[i])
+
     for k in range(3):
         wait(Xs.at[pl.ds(0, ns - 1)], sV.at[k])
     wait(Gt.at[:, pl.ds(0, (2 * nzl - 1) * B)], sG)
@@ -426,6 +438,7 @@
 
     wait(wout, sO.at[1])
     wait(Wo.at[pl.ds(0, 2 * B), pl.ds(0, (ny - 1) * B)], sO.at[2])
+    sides = Wo.at[pl.ds(0, 2 * B)]
     wait(sides, sO.at[3])
     if nx > 2:
         wait(sides, sO.at[4])
@@ -456,6 +469,9 @@
             pltpu.VMEM((np_ * B, 3 * B), BF16),
             pltpu.VMEM((ny, B, 3 * B), BF16),
             pltpu.VMEM((ny, B, 3 * B), BF16),
+            pltpu.VMEM((2, B, 3 * B), F32),
+            pltpu.VMEM((2, B, 3 * B), F32),
+            pltpu.VMEM((ny, HALO, 3 * B), BF16),
             pltpu.VMEM((ny, HALO, 3 * B), BF16),
             pltpu.VMEM((HALO + B, 3 * B), F32),
             pltpu.VMEM((2, B, B), F32),
@@ -472,11 +488,11 @@
             dma, dma((ny,)),
             dma, dma((ny,)),
             dma, dma((ny,)),
-            dma, dma,
+            dma((ny,)), dma((ny,)), dma((2,)),
             dma((ny,)), dma,
             dma((3,)), dma((3,)),
             dma, dma((2,)),
-            dma((6,)), dma((6,)), dma((ny,)), dma((ny,)),
+            dma((6,)), dma((6,)), dma((ny,)), dma((ny,)), dma((ny,)), dma((ny,)),
         ],
         compiler_params=pltpu.CompilerParams(
             collective_id=0, has_side_effects=True

time: 98.5 us -> 91.2 us (0.926)
  Pallas kernels: 96.7 us -> 89.4 us
    pallas_call x1, Pallas kernels: 96.7 us -> 89.4 us  [per_device(): pl.pallas_call(functools.partial(kernel, ny, nx), out_shape=jax.ShapeDtyp...]
where the time goes in v4:
time: 91.2 us; the launch traced here: 91 us
  Pallas kernels  89.4 us (98%)
  local copies, waits for them, and re-layouts  1.67 us (2%)
    pallas_call x1, Pallas kernels, per_device(): pl.pallas_call(functools.partial(kernel, ny, nx), out_shape=jax.ShapeDtyp...  89.4 us

profile of v4, /device:TPU:1, one launch (start us, length us, event | category | flops | bytes accessed | tf_op | source)
XLA Modules:
  0.0 91.0 jit_solution(6019368632352980394)
XLA Ops:
  0.0 89.4 %operator.1 = bf16[128,1024]{1,0:T(8,128)(2,1)} custom-call(bf16[128,1024]{1,0:T(8,128)(2,1)} %feat_h.1, bf16[3,128,128]{2,1,0:T(8,128)(2,1)} %win_h.1, f32[3,3,128]{2,1,0:T(4,128)} %taps_h.1, f32[128,128]{1,0:T(8,128)} %filt_h.1, f32[1,128]{1,0:T(1,128)} %bitcast.1, bf16[128,128]{1,0:T(8,128)(2,1)} %wout_h.1), custom_call_target="tpu_custom_call" | custom-call | tf_op jit(solution)/shard_map/operator/pallas_call | solution.py:455
  89.4 1.7 %copy.8 = bf16[128,1024]{1,0:T(8,128)(2,1)} copy(bf16[128,1024]{1,0:T(8,128)(2,1)} %operator.1) | data formatting | bytes 524288

commit v5 on v4

--- a/solution.py
+++ b/solution.py
@@ -20,7 +20,7 @@
     ny, nx, feat_h, win_h, taps_h, filt_h, skip_h, wout_h, out,
     feat, win, taps, filt, skip, wout,
     F, Wb, Wc, Ps, Pr, Pf, Pe, Hs, Hr, pad, qi, Fs, Fr, Xs, Xr, Ys, Yr, Xp, A, T, Gs, Gt, Wo,
-    arg, loc, sF, rF, sW, rW, sZ, rZ, sE, rE, sC, rC, sP, rP, rN, sH, rH, sV, rV, sG, rG, sO, rO, rU, rD, rR, rL,
+    arg, loc, sF, rF, sW, rW, sZ, rZ, sE, rE, sC, rC, sP, rP, rN, sH, rH, sV, rV, sG, rG, sO, rO, rU, rD, rR, rL, round_y, round_x,
 ):
     np_ = 2 * nx
     nq = 2 * nx
@@ -68,14 +68,27 @@
             barrier, inc=1, device_id={"seq": sq, "tp": tp}, device_id_type=pl.DeviceIdType.MESH
         )
 
-    loop(0, ns - 1, lambda k: greet(away(k), p))
+    x_pos = q % nx
+
+    def x_line(k):
+        return ((q - x_pos) + (x_pos + k) % nx) * ny + y
+
+    def y_line(k):
+        return q * ny + (y + k) % ny
+
     greet(p * ny + y, far)
+    greet(far * ny + y, p)
+    for k in range(1, ny):
+        greet(y_line(k), p)
+    for k in range(1, nx):
+        greet(x_line(k), p)
 
     @pl.when(q != p)
     def _():
         greet(p * ny + y, q)
 
-    loop(1, np_, lambda k: greet(s, (p + k) % np_))
+    for k in range(1, np_):
+        greet(s, (p + k) % np_)
 
     wait(feat, arg.at[1])
     wait(win, arg.at[2])
@@ -101,7 +114,12 @@
     def _():
         wait(wout, loc.at[2])
 
-    pl.semaphore_wait(barrier, ns + np_ - 1 + jnp.where(q == p, 0, 1))
+    pl.semaphore_wait(barrier, 2 + ny - 1 + nx - 1 + np_ - 1 + jnp.where(q == p, 0, 1))
+
+    def tell(sem, sq):
+        pl.semaphore_signal(
+            sem, inc=1, device_id={"seq": sq, "tp": p}, device_id_type=pl.DeviceIdType.MESH
+        )
 
     reach = ny // 2
 
@@ -190,6 +208,9 @@
 
     weights(q, rW.at[1])
 
+    for k in range(1, ny):
+        tell(round_y, y_line(k))
+
     @pl.when(q != p)
     def _():
         send(wout, Wo.at[lanes(p), lanes(y)], sO.at[0], rO.at[0], p * ny + y, q)
@@ -199,13 +220,15 @@
         pass_on(i)
     wait(Wb.at[0], rW.at[0])
     weights(far, rW.at[2])
+    pl.semaphore_wait(round_y, ny - 1)
+    for k in range(1, nx):
+        tell(round_x, x_line(k))
 
     @pl.when(q != p)
     def _():
         wait(wout, rO.at[0])
 
     wait(wout, rO.at[1])
-    x_pos = q % nx
     right = ((q - x_pos) + (x_pos + 1) % nx) * ny + y
     left = ((q - x_pos) + (x_pos + nx - 1) % nx) * ny + y
 
@@ -253,6 +276,7 @@
             send(piece(q, t), piece(q, t), sO.at[2], rD.at[reach + t], near(-1), p)
 
     ring(0)
+    pl.semaphore_wait(round_x, nx - 1)
     loop(0, ns - 1, lambda k: send(Fs.at[away(k)], Fr.at[s], sV.at[0], rV.at[0], away(k), p))
 
     row = lax.broadcasted_iota(jnp.int32, (B, B), 0)
@@ -325,14 +349,11 @@
         relay(block_of(i))
         if i >= 1:
             last_leg(block_of(i - 1))
-        if i >= 2:
-            project(i - 2)
+            project(i - 1)
         if i % 2 == 1 and i // 2 + 1 <= reach:
             ring(i // 2 + 1)
             across(i // 2)
     last_leg(block_of(ny - 2))
-    if ny > 2:
-        project(ny - 3)
     project(ny - 2)
     ring(reach)
     across(reach - 1)
@@ -391,17 +412,17 @@
 
     gated = Gt.at[:, lanes(p)]
     for k in range(1, nzl):
-        send(Gs, gated, sG, rG.at[0], s, ((zl + k) % nzl) * 2 + c)
-    send(Gs, gated, sG, rG.at[1], s, mate)
+        send(Gs, gated, sG, rG.at[nzl - k], s, ((zl + k) % nzl) * 2 + c)
+    send(Gs, gated, sG, rG.at[0], s, mate)
     local(Gs, gated, loc.at[0])
     if nx > 2:
         wait(Wo.at[pl.ds(0, 2 * B)], rO.at[5])
     wait(Gs, loc.at[0])
-    wait(Gt.at[:, pl.ds(0, (nzl - 1) * B)], rG.at[0])
-    for k in range(1, nzl):
+    for k in sorted(range(1, nzl), key=lambda k: min(k, nzl - k)):
         other = Gt.at[:, lanes(((zl + k) % nzl) * 2 + c)]
-        send(other, other, sG, rG.at[1], s, mate)
-    wait(Gt.at[:, pl.ds(0, nzl * B)], rG.at[1])
+        wait(Gs, rG.at[k])
+        send(other, other, sG, rG.at[0], s, mate)
+    wait(Gt.at[:, pl.ds(0, nzl * B)], rG.at[0])
     out[...] = jnp.dot(Gt[...], Wo[...], preferred_element_type=F32).astype(BF16)
 
     wait(F.at[pl.ds(0, ny - 1), :, pl.ds(0, B)], sF)
@@ -491,8 +512,9 @@
             dma((ny,)), dma((ny,)), dma((2,)),
             dma((ny,)), dma,
             dma((3,)), dma((3,)),
-            dma, dma((2,)),
+            dma, dma((max(2, np_ // 2),)),
             dma((6,)), dma((6,)), dma((ny,)), dma((ny,)), dma((ny,)), dma((ny,)),
+            pltpu.SemaphoreType.REGULAR, pltpu.SemaphoreType.REGULAR,
         ],
         compiler_params=pltpu.CompilerParams(
             collective_id=0, has_side_effects=True

time: 91.2 us -> 86.9 us (0.953)
  Pallas kernels: 89.4 us -> 85.1 us
    pallas_call x1, Pallas kernels: 89.4 us -> 85.1 us  [per_device(): pl.pallas_call(functools.partial(kernel, ny, nx), out_shape=jax.ShapeDtyp...]
where the time goes in v5:
time: 86.9 us; the launch traced here: 86.7 us
  Pallas kernels  85.1 us (98%)
  local copies, waits for them, and re-layouts  1.67 us (2%)
    pallas_call x1, Pallas kernels, per_device(): pl.pallas_call(functools.partial(kernel, ny, nx), out_shape=jax.ShapeDtyp...  85.1 us

profile of v5, /device:TPU:1, one launch (start us, length us, event | category | flops | bytes accessed | tf_op | source)
XLA Modules:
  0.0 86.7 jit_solution(8010249079782351373)
XLA Ops:
  0.0 85.1 %operator.1 = bf16[128,1024]{1,0:T(8,128)(2,1)} custom-call(bf16[128,1024]{1,0:T(8,128)(2,1)} %feat_h.1, bf16[3,128,128]{2,1,0:T(8,128)(2,1)} %win_h.1, f32[3,3,128]{2,1,0:T(4,128)} %taps_h.1, f32[128,128]{1,0:T(8,128)} %filt_h.1, f32[1,128]{1,0:T(1,128)} %bitcast.1, bf16[128,128]{1,0:T(8,128)(2,1)} %wout_h.1), custom_call_target="tpu_custom_call" | custom-call | tf_op jit(solution)/shard_map/operator/pallas_call | solution.py:476
  85.1 1.7 %copy.8 = bf16[128,1024]{1,0:T(8,128)(2,1)} copy(bf16[128,1024]{1,0:T(8,128)(2,1)} %operator.1) | data formatting | bytes 524288

commit v6 on v5

--- a/solution.py
+++ b/solution.py
@@ -52,7 +52,7 @@
         lax.fori_loop(lo, hi, lambda i, carry: (body(i), carry)[1], 0)
 
     def away(k):
-        return (s + (k + ns // 3) % (ns - 1) + 1) % ns
+        return lax.rem(s + lax.rem(k + ns // 3, ns - 1) + 1, ns)
 
     local(filt_h, filt, arg.at[0])
     local(feat_h, feat, arg.at[1])
@@ -99,20 +99,6 @@
     @pl.when(q == p)
     def _():
         local(wout, Wo.at[lanes(q), lanes(y)], loc.at[2])
-
-    wait(filt, arg.at[0])
-    turned = filt[...].T
-    for k in range(cpd):
-        Fs[:, k, :] = turned[k * ns:(k + 1) * ns]
-    Fr[pl.ds(s, 1)] = Fs[pl.ds(s, 1)]
-    wait(taps, arg.at[4])
-    wait(skip, arg.at[5])
-    wait(F.at[0, :, pl.ds(0, B)], loc.at[0])
-    wait(win, loc.at[1])
-
-    @pl.when(q == p)
-    def _():
-        wait(wout, loc.at[2])
 
     pl.semaphore_wait(barrier, 2 + ny - 1 + nx - 1 + np_ - 1 + jnp.where(q == p, 0, 1))
 
@@ -196,7 +182,9 @@
     for i in range(ny - 1):
         spread(i)
     send(win, Wb.at[q], sW, rW.at[0], far * ny + y, p)
+    wait(F.at[0, :, pl.ds(0, B)], loc.at[0])
     forward(y)
+    wait(win, loc.at[1])
 
     def weights(which, sem):
         def step(k):
@@ -223,6 +211,10 @@
     pl.semaphore_wait(round_y, ny - 1)
     for k in range(1, nx):
         tell(round_x, x_line(k))
+
+    @pl.when(q == p)
+    def _():
+        wait(wout, loc.at[2])
 
     @pl.when(q != p)
     def _():
@@ -276,6 +268,13 @@
             send(piece(q, t), piece(q, t), sO.at[2], rD.at[reach + t], near(-1), p)
 
     ring(0)
+    wait(filt, arg.at[0])
+    turned = filt[...].T
+    for k in range(cpd):
+        Fs[:, k, :] = turned[k * ns:(k + 1) * ns]
+    Fr[pl.ds(s, 1)] = Fs[pl.ds(s, 1)]
+    wait(taps, arg.at[4])
+    wait(skip, arg.at[5])
     pl.semaphore_wait(round_x, nx - 1)
     loop(0, ns - 1, lambda k: send(Fs.at[away(k)], Fr.at[s], sV.at[0], rV.at[0], away(k), p))
 
@@ -350,17 +349,24 @@
         if i >= 1:
             last_leg(block_of(i - 1))
             project(i - 1)
-        if i % 2 == 1 and i // 2 + 1 <= reach:
-            ring(i // 2 + 1)
-            across(i // 2)
+        if i == 1 and reach > 2:
+            ring(1)
+        if i == 4:
+            ring(2)
+            across(0)
     last_leg(block_of(ny - 2))
     project(ny - 2)
-    ring(reach)
-    across(reach - 1)
+    early = 2 if reach > 2 else 0
+    if early:
+        ring(3)
+        across(1)
     project(ny - 1)
     wait(Fr.at[pl.ds(0, ns - 1)], rV.at[0])
     loop(0, 8, toeplitz)
-    across(reach)
+    for t in range(early + 2 if early else 1, reach + 1):
+        ring(t)
+    if early:
+        across(2)
 
     full = pad[HALO:]
     for side in range(2 if ny > 2 else 1):
@@ -397,6 +403,8 @@
     Xr[pl.ds(s, 1)] = Xs[pl.ds(s, 1)]
     loop(0, ns - 1, lambda k: send(Xs.at[away(k)], Xr.at[s], sV.at[1], rV.at[1], away(k), p))
     Xp[:ns] = jnp.zeros((ns, B), F32)
+    for t in range(early + 1 if early else 0, reach + 1):
+        across(t)
 
     wait(Xr.at[pl.ds(0, ns - 1)], rV.at[1])
     for ch in range(cpd):

time: 86.9 us -> 86.2 us (level)
  no operation moved by 1% of the time
where the time goes in v6:
time: 86.2 us; the launch traced here: 86 us
  Pallas kernels  84.3 us (98%)
  local copies, waits for them, and re-layouts  1.67 us (2%)
    pallas_call x1, Pallas kernels, per_device(): pl.pallas_call(functools.partial(kernel, ny, nx), out_shape=jax.ShapeDtyp...  84.3 us

profile of v6, /device:TPU:1, one launch (start us, length us, event | category | flops | bytes accessed | tf_op | source)
XLA Modules:
  0.0 86.0 jit_solution(11440799686174908398)
XLA Ops:
  0.0 84.3 %operator.1 = bf16[128,1024]{1,0:T(8,128)(2,1)} custom-call(bf16[128,1024]{1,0:T(8,128)(2,1)} %feat_h.1, bf16[3,128,128]{2,1,0:T(8,128)(2,1)} %win_h.1, f32[3,3,128]{2,1,0:T(4,128)} %taps_h.1, f32[128,128]{1,0:T(8,128)} %filt_h.1, f32[1,128]{1,0:T(1,128)} %bitcast.1, bf16[128,128]{1,0:T(8,128)(2,1)} %wout_h.1), custom_call_target="tpu_custom_call" | custom-call | tf_op jit(solution)/shard_map/operator/pallas_call | solution.py:484
  84.3 1.7 %copy.8 = bf16[128,1024]{1,0:T(8,128)(2,1)} copy(bf16[128,1024]{1,0:T(8,128)(2,1)} %operator.1) | data formatting | bytes 524288

commit v7 on v6

--- a/solution.py
+++ b/solution.py
@@ -363,10 +363,6 @@
     project(ny - 1)
     wait(Fr.at[pl.ds(0, ns - 1)], rV.at[0])
     loop(0, 8, toeplitz)
-    for t in range(early + 2 if early else 1, reach + 1):
-        ring(t)
-    if early:
-        across(2)
 
     full = pad[HALO:]
     for side in range(2 if ny > 2 else 1):
@@ -403,7 +399,9 @@
     Xr[pl.ds(s, 1)] = Xs[pl.ds(s, 1)]
     loop(0, ns - 1, lambda k: send(Xs.at[away(k)], Xr.at[s], sV.at[1], rV.at[1], away(k), p))
     Xp[:ns] = jnp.zeros((ns, B), F32)
-    for t in range(early + 1 if early else 0, reach + 1):
+    for t in range(early + 2 if early else 1, reach + 1):
+        ring(t)
+    for t in range(early, reach + 1):
         across(t)
 
     wait(Xr.at[pl.ds(0, ns - 1)], rV.at[1])

time: 86.2 us -> 86.1 us (level)
  no operation moved by 1% of the time
where the time goes in v7:
time: 86.1 us; the launch traced here: 86 us
  Pallas kernels  84.3 us (98%)
  local copies, waits for them, and re-layouts  1.67 us (2%)
    pallas_call x1, Pallas kernels, per_device(): pl.pallas_call(functools.partial(kernel, ny, nx), out_shape=jax.ShapeDtyp...  84.3 us

profile of v7, /device:TPU:1, one launch (start us, length us, event | category | flops | bytes accessed | tf_op | source)
XLA Modules:
  0.0 86.0 jit_solution(15465015464326060543)
XLA Ops:
  0.0 84.3 %operator.1 = bf16[128,1024]{1,0:T(8,128)(2,1)} custom-call(bf16[128,1024]{1,0:T(8,128)(2,1)} %feat_h.1, bf16[3,128,128]{2,1,0:T(8,128)(2,1)} %win_h.1, f32[3,3,128]{2,1,0:T(4,128)} %taps_h.1, f32[128,128]{1,0:T(8,128)} %filt_h.1, f32[1,128]{1,0:T(1,128)} %bitcast.1, bf16[128,128]{1,0:T(8,128)(2,1)} %wout_h.1), custom_call_target="tpu_custom_call" | custom-call | tf_op jit(solution)/shard_map/operator/pallas_call | solution.py:482
  84.3 1.7 %copy.8 = bf16[128,1024]{1,0:T(8,128)(2,1)} copy(bf16[128,1024]{1,0:T(8,128)(2,1)} %operator.1) | data formatting | bytes 524288

commit v8 on v5

--- a/solution.py
+++ b/solution.py
@@ -49,10 +49,11 @@
         pltpu.make_async_copy(src, dst, sem).start()
 
     def loop(lo, hi, body):
-        lax.fori_loop(lo, hi, lambda i, carry: (body(i), carry)[1], 0)
+        unroll = 7 if hi == ns - 1 else 1
+        lax.fori_loop(lo, hi, lambda i, carry: (body(i), carry)[1], 0, unroll=unroll)
 
     def away(k):
-        return (s + (k + ns // 3) % (ns - 1) + 1) % ns
+        return lax.rem(s + lax.rem(k + ns // 3, ns - 1) + 1, ns)
 
     local(filt_h, filt, arg.at[0])
     local(feat_h, feat, arg.at[1])

time: 86.9 us -> 85.3 us (0.982)
  Pallas kernels: 85.1 us -> 83.5 us
    pallas_call x1, Pallas kernels: 85.1 us -> 83.5 us  [per_device(): pl.pallas_call(functools.partial(kernel, ny, nx), out_shape=jax.ShapeDtyp...]
where the time goes in v8:
time: 85.3 us; the launch traced here: 85.2 us
  Pallas kernels  83.5 us (98%)
  local copies, waits for them, and re-layouts  1.67 us (2%)
    pallas_call x1, Pallas kernels, per_device(): pl.pallas_call(functools.partial(kernel, ny, nx), out_shape=jax.ShapeDtyp...  83.5 us

profile of v8, /device:TPU:1, one launch (start us, length us, event | category | flops | bytes accessed | tf_op | source)
XLA Modules:
  0.0 85.2 jit_solution(7550923366622797891)
XLA Ops:
  0.0 83.5 %operator.1 = bf16[128,1024]{1,0:T(8,128)(2,1)} custom-call(bf16[128,1024]{1,0:T(8,128)(2,1)} %feat_h.1, bf16[3,128,128]{2,1,0:T(8,128)(2,1)} %win_h.1, f32[3,3,128]{2,1,0:T(4,128)} %taps_h.1, f32[128,128]{1,0:T(8,128)} %filt_h.1, f32[1,128]{1,0:T(1,128)} %bitcast.1, bf16[128,128]{1,0:T(8,128)(2,1)} %wout_h.1), custom_call_target="tpu_custom_call" | custom-call | tf_op jit(solution)/shard_map/operator/pallas_call | solution.py:477
  83.5 1.7 %copy.8 = bf16[128,1024]{1,0:T(8,128)(2,1)} copy(bf16[128,1024]{1,0:T(8,128)(2,1)} %operator.1) | data formatting | bytes 524288
